TPU v7x, 32 devices: a whole 2x2x4 slice. The times are simulated.
32 devices in a mesh: groups: 2 (over y), blk: 4 (over z), dp: 2 (over x), sub: 2 (over core).
Axes of the slice: x: 2, y: 2, z: 4, core: 2. Of those that a mesh axis runs over, the one named last changes fastest.
Arguments:
- cls_feats: bfloat16 [4096, 1024], P(('groups', 'blk', 'dp', 'sub')), parts along dimension 0, may hold values from -6 to 6
- proj: bfloat16 [1024, 768], replicated, may hold values from -0.1875 to 0.1875
- cluster_id: int32 [4096, 1], P(('groups', 'blk', 'dp', 'sub')), parts along dimension 0, may hold values from 0 to 7; in each aligned block of 128 rows (0 to 127, 128 to 255, ...) at most 32 rows name the same one
- row_index: int32 [4096], P(('groups', 'blk', 'dp', 'sub')), parts along dimension 0, may hold values from 0 to 2047, each once
- assign: int32 [16], P('groups'), parts along dimension 0, may hold values from 0 to 7, each once
Outputs:
- best_cos: float32 [4096], P(('groups', 'blk', 'dp', 'sub')), parts along dimension 0
There are 2 independent parts, one for each index of `groups`. A program takes and returns all parts, laid end to end along the dimension named above; an argument that names none is the same for every part. Nothing has to cross between parts.
Inputs may be any that keep to these rules, and one draw needn't show every extreme that they name: `cluster_id`: among the 128 images of one device, at most 32 lie in one fine cluster; some device has exactly 32 in some fine cluster, and every fine cluster has some image. `row_index`: every number appears once. `assign`: every number appears once.
All inputs are finite; a program needn't handle non-finite values.
Results may differ from a plain program's by a relative error of at most 0.0015.
Values may be sent and summed in bfloat16 or wider, within the bound.
No kernel may reach another device: no remote copies, remote signals or barrier semaphores. Data moves between devices by JAX's collectives and lax.ppermute only.
A program may use at most 64 MiB of HBM per device.

v0:
```python
import math

import jax
import jax.numpy as jnp
from jax import lax
from jax.sharding import PartitionSpec as P

empty_mark = 2**30


def fold_best(carry, piece, row_emb, row_idx):
    col_emb, col_idx = piece
    count = col_emb.shape[0]
    width = math.gcd(count, 1024)
    blocks = count // width
    col_blocks = col_emb.reshape(blocks, width, col_emb.shape[1])
    idx_blocks = col_idx.reshape(blocks, width)

    def step(best, pair):
        block_emb, block_idx = pair
        scores = lax.dot_general(
            row_emb, block_emb, (((1,), (1,)), ((), ())), preferred_element_type=jnp.float32
        )
        scores = jnp.where(block_idx[None, :] < row_idx[:, None], scores, -1.0)
        return (jnp.maximum(best, jnp.max(scores, axis=1)), None)

    best, _ = lax.scan(step, carry, (col_blocks, idx_blocks))
    return best


def local(cls_feats, proj, cluster_id, row_index, assign):
    rows = cls_feats.shape[0]
    feats = cls_feats.astype(jnp.float32)
    center = jnp.mean(feats, axis=1, keepdims=True)
    spread = jnp.mean((feats - center) ** 2, axis=1, keepdims=True)
    normed = ((feats - center) * lax.rsqrt(spread + 1e-05)).astype(jnp.bfloat16)
    proj_out = jnp.dot(normed, proj, preferred_element_type=jnp.float32)
    scale = lax.rsqrt(jnp.sum(proj_out * proj_out, axis=1, keepdims=True) + 1e-06)
    emb = (proj_out * scale).astype(jnp.bfloat16)
    width = emb.shape[1]
    fine_count = assign.shape[0]
    most_fine = 2 * rows // fine_count
    slots = fine_count * most_fine
    onehot = cluster_id == jnp.arange(fine_count, dtype=jnp.int32)[None, :]
    counts = onehot.astype(jnp.int32)
    earlier = jnp.cumsum(counts, axis=0) - counts
    rank = jnp.sum(jnp.where(onehot, earlier, 0), axis=1)
    base = jnp.sum(jnp.where(onehot, assign[None, :], 0), axis=1)
    slot = base * most_fine + rank
    place = slot[None, :] == jnp.arange(slots, dtype=jnp.int32)[:, None]
    send_emb = jnp.dot(place.astype(jnp.bfloat16), emb, preferred_element_type=jnp.float32).astype(
        jnp.bfloat16
    )
    filled = jnp.any(place, axis=1)
    send_idx = jnp.where(
        filled, jnp.sum(jnp.where(place, row_index[None, :], 0), axis=1), empty_mark
    )
    n_groups = lax.axis_size("dp")
    per_group = slots // n_groups
    recv_emb, recv_idx = (
        lax.all_to_all(
            send_emb.reshape(n_groups, per_group, width),
            "dp",
            split_axis=0,
            concat_axis=0,
            tiled=True,
        ),
        lax.all_to_all(
            send_idx.reshape(n_groups, per_group), "dp", split_axis=0, concat_axis=0, tiled=True
        ),
    )
    own_emb = recv_emb.reshape(slots, width)
    own_idx = recv_idx.reshape(slots)
    both_emb, both_idx = (
        lax.all_gather(own_emb, "sub", axis=0, tiled=True),
        lax.all_gather(own_idx, "sub", axis=0, tiled=True),
    )
    start_best = jnp.full((2 * slots,), -1.0, jnp.float32)
    partial_best = fold_best(
        start_best,
        (
            lax.all_gather(own_emb, "blk", axis=0, tiled=True),
            lax.all_gather(own_idx, "blk", axis=0, tiled=True),
        ),
        both_emb,
        both_idx,
    )
    joined = lax.pmax(partial_best, "sub")
    best = lax.dynamic_slice_in_dim(joined, lax.axis_index("sub") * slots, slots, 0)
    back = lax.all_to_all(
        best.reshape(n_groups, per_group), "dp", split_axis=0, concat_axis=0, tiled=True
    )
    flat = back.reshape(slots)
    return jnp.dot(flat, place.astype(jnp.float32), precision=lax.Precision.HIGHEST)


def solution(mesh):
    in_specs = (
        P(("groups", "blk", "dp", "sub"), None),
        P(),
        P(("groups", "blk", "dp", "sub"), None),
        P(("groups", "blk", "dp", "sub")),
        P("groups"),
    )
    out_specs = P(("groups", "blk", "dp", "sub"))
    return jax.shard_map(local, mesh=mesh, in_specs=in_specs, out_specs=out_specs, check_vma=False)
```

profile of v0, /device:TPU:0, one launch (start us, length us, event | category | flops | bytes accessed | tf_op | source)
XLA Modules:
  0.0 79.7 jit_solution(8569290460033763673)
XLA Ops:
  6.5 0.0 copy-start
  6.5 0.0 copy-start.1
  6.5 0.0 copy-start.2
  6.5 0.0 all-gather.4.cloned.1.call-start
  6.5 0.9 %fusion.12 = s32[128,8]{1,0:T(8,128)S(1)} fusion(s32[128]{0:T(128)} %bitcast.25), kind=kLoop, calls=%fused_computation.23 | loop fusion | flops 2048 | bytes 4608 | tf_op jit(solution)/shard_map/convert_element_type | solution.py:45
  7.4 1.1 %convert_reduce_fusion = f32[128]{0:T(128)S(1)} fusion(bf16[128,1024]{1,0:T(8,128)(2,1)} %param.5), kind=kLoop, calls=%fused_computation.4 | loop fusion | flops 262016 | bytes 262656 | tf_op jit(solution)/shard_map/reduce_sum | solution.py:34
  8.5 1.2 %fusion.2 = f32[128]{0:T(128)S(1)} fusion(bf16[128,1024]{1,0:T(8,128)(2,1)} %param.5, f32[128]{0:T(128)S(1)} %broadcast_multiply_fusion), kind=kLoop, calls=%fused_computation.7 | loop fusion | flops 524160 | bytes 263168 | tf_op jit(solution)/shard_map/reduce_sum | solution.py:35
  9.7 0.0 copy-done
  9.7 1.4 %multiply_reduce_fusion = (f32[128]{0:T(128)S(1)}, f32[128,768]{1,0:T(8,128)S(1)}) fusion(bf16[1024,768]{1,0:T(8,128)(2,1)S(1)} %copy-done, bf16[128,1024]{1,0:T(8,128)(2,1)} %param.5, f32[128]{0:T(128)S(1)} %add_rsqrt_fusion.1, f32[128]{0:T(128)S(1)} %broadcast_multiply_fusion), kind=kOutput, calls=%fused_computation.10 | convolution fusion | flops 202047360 | bytes 2229760 | tf_op jit(solution)/shard_map/dot_general | solution.py:37
  11.1 0.0 copy-start.3
  11.1 0.2 reduce_window_sum.11
  11.3 0.0 copy-done.1
  11.3 0.0 copy-done.2
  11.3 0.2 select_reduce_fusion.3
  11.5 0.3 convolution_convert_fusion
  11.8 11.2 %all_to_all.20 = bf16[2,128,768]{2,1,0:T(8,128)(2,1)} all-to-all(bf16[2,128,768]{2,1,0:T(8,128)(2,1)S(1)} %bitcast.20), channel_id=1, replica_groups=mesh['groups'=2,'blk'=4,'dp'=2,'sub'=2] {'dp'}, dimensions={0} | all-to-all | bytes 786432 | tf_op jit(solution)/shard_map/all_to_all | solution.py:61
  23.0 0.0 all-gather.4.cloned.1.call-update
  23.1 0.1 fusion.9
  23.2 0.0 copy-done.3
  23.2 0.1 select_reduce_fusion.1
  23.3 0.6 broadcast_select_fusion
  23.9 3.2 %all-to-all-start = ((s32[2,1,128]{2,1,0:T(1,128)}), s32[2,1,128]{2,1,0:T(1,128)S(1)}, u32[]{:S(2)}, u32[]{:S(2)}) async-start(s32[2,1,128]{2,1,0:T(1,128)} %bitcast.1), calls=%async_computation | async-start | bytes 2048 | tf_op jit(solution)/shard_map/all_to_all | solution.py:68
  27.1 3.8 %all-to-all-done = s32[2,1,128]{2,1,0:T(1,128)S(1)} async-done(((s32[2,1,128]{2,1,0:T(1,128)}), s32[2,1,128]{2,1,0:T(1,128)S(1)}, u32[]{:S(2)}, u32[]{:S(2)}) %all-to-all-start) | async-done | bytes 1056 | tf_op jit(solution)/shard_map/all_to_all | solution.py:68
  30.8 1.8 %all-gather.1 = s32[2,1,256]{2,1,0:T(1,128)S(1)} all-gather(s32[1,1,256]{2,1,0:T(1,128)S(1)} %bitcast.21), channel_id=1, replica_groups=mesh['groups'=2,'blk'=4,'dp'=2,'sub'=2] {'sub'}, dimensions={0}, use_global_device_ids=true | all-gather | bytes 3072 | tf_op jit(solution)/shard_map/all_gather | solution.py:76
  32.6 11.8 %all-gather = s32[4,1,256]{2,1,0:T(1,128)S(1)} all-gather(s32[1,1,256]{2,1,0:T(1,128)S(1)} %bitcast.22), channel_id=1, replica_groups=mesh['groups'=2,'blk'=4,'dp'=2,'sub'=2] {'blk'}, dimensions={0}, use_global_device_ids=true | all-gather | bytes 5120 | tf_op jit(solution)/shard_map/all_gather | solution.py:83
  44.4 2.6 %all_gather.14 = bf16[512,768]{1,0:T(8,128)(2,1)S(1)} all-gather(bf16[256,768]{1,0:T(8,128)(2,1)} %bitcast.19), channel_id=1, replica_groups=mesh['groups'=2,'blk'=4,'dp'=2,'sub'=2] {'sub'}, dimensions={0}, use_global_device_ids=true | all-gather | bytes 1179648 | tf_op jit(solution)/shard_map/all_gather | solution.py:75
  47.0 13.9 %all-gather.4.cloned.1.call-done = bf16[1024,768]{1,0:T(8,128)(2,1)} async-done(((bf16[256,768]{1,0:T(8,128)(2,1)}), bf16[1024,768]{1,0:T(8,128)(2,1)}) %all-gather.4.cloned.1.call-update) | async-done | bytes 1572880 | tf_op jit(solution)/shard_map/all_gather | solution.py:82
  60.9 2.5 %select_reduce_fusion = f32[512]{0:T(512)S(1)} fusion(bf16[512,768]{1,0:T(8,128)(2,1)S(1)} %all_gather.14, bf16[1024,768]{1,0:T(8,128)(2,1)} %all-gather.4.cloned.1.call-done, s32[1024]{0:T(1024)S(1)} %bitcast.23, s32[512]{0:T(512)S(1)} %bitcast.27), kind=kOutput, calls=%fused_computation | convolution fusion | flops 806878720 | bytes 2367488 | tf_op jit(solution)/shard_map/while/body/eval_jaxpr/dot_general | solution.py:21
  63.4 2.5 %pmax.7 = f32[512]{0:T(512)S(1)} all-reduce(f32[512]{0:T(512)S(1)} %broadcast_maximum_fusion), channel_id=1, replica_groups=mesh['groups'=2,'blk'=4,'dp'=2,'sub'=2] {'sub'}, use_global_device_ids=true, to_apply=%region_9.10 | all-reduce | flops 512 | bytes 4096 | tf_op jit(solution)/shard_map/pmax | solution.py:88
  65.8 0.1 dynamic_slice.9
  65.9 6.3 %all_to_all.21 = f32[2,1,128]{2,1,0:T(1,128)S(1)} all-to-all(f32[2,1,128]{2,1,0:T(1,128)S(1)} %bitcast.24), channel_id=1, replica_groups=mesh['groups'=2,'blk'=4,'dp'=2,'sub'=2] {'dp'}, dimensions={0} | all-to-all | bytes 2048 | tf_op jit(solution)/shard_map/all_to_all | solution.py:90
  72.2 0.7 convolution_bitcast_fusion
  (5 shorter events, 0.0 us)
Async XLA Ops:
  6.5 3.1 %copy-start = (bf16[1024,768]{1,0:T(8,128)(2,1)S(1)}, bf16[1024,768]{1,0:T(8,128)(2,1)}, u32[]{:S(2)}) copy-start(bf16[1024,768]{1,0:T(8,128)(2,1)} %param.6) | copy-start | bytes 4718596
  6.5 4.8 %copy-start.1 = (s32[128,1]{0,1:T(1,128)S(1)}, s32[128,1]{0,1:T(1,128)}, u32[]{:S(2)}) copy-start(s32[128,1]{0,1:T(1,128)} %param.7) | copy-start | bytes 1540
  6.5 4.8 %copy-start.2 = (s32[8]{0:T(128)S(1)}, s32[8]{0:T(128)}, u32[]{:S(2)}) copy-start(s32[8]{0:T(128)} %param.9) | copy-start | bytes 100
  6.5 54.3 %all-gather.4.cloned.1.call-start = ((), (), s32[]{:S(2)}) async-start(), calls=%async_computation.3 | async-start | bytes 1966080 | tf_op jit(solution)/shard_map/all_gather | solution.py:82
  11.1 12.1 %copy-start.3 = (s32[128]{0:T(128)S(1)}, s32[128]{0:T(128)}, u32[]{:S(2)}) copy-start(s32[128]{0:T(128)} %param.8) | copy-start | bytes 1540
  23.9 6.9 %all-to-all-start = ((s32[2,1,128]{2,1,0:T(1,128)}), s32[2,1,128]{2,1,0:T(1,128)S(1)}, u32[]{:S(2)}, u32[]{:S(2)}) async-start(s32[2,1,128]{2,1,0:T(1,128)} %bitcast.1), calls=%async_computation | async-start | bytes 2048 | tf_op jit(solution)/shard_map/all_to_all | solution.py:68
Sparse Core Ops, SparseCore 0:
  23.2 37.6 all-gather.3
where the time goes:
time: 80.1 us; the launch traced here: 79.7 us
  blocking collectives  36.1 us (45%)
  waiting for transfers between devices  17.6 us (22%)
  between operations  13.5 us (17%)
  matrix products  4.94 us (6%)
  other arithmetic  4.3 us (5%)
  starting transfers between devices  3.16 us (4%)
    all_gather x1, waiting for transfers between devices, local(): lax.all_gather(own_emb, 'blk', axis=0, tiled=True)  13.9 us
    all_gather x1, blocking collectives, local(): lax.all_gather(own_idx, 'blk', axis=0, tiled=True)  11.8 us
    all_to_all x1, blocking collectives, local(): lax.all_to_all(send_emb.reshape(n_groups, per_group, width), 'dp', split_...  11.2 us
    all_to_all x1, blocking collectives, local(): lax.all_to_all(best.reshape(n_groups, per_group), 'dp', split_axis=0, con...  6.3 us
    all_to_all x1, waiting for transfers between devices, local(): lax.all_to_all(send_idx.reshape(n_groups, per_group), 'dp', split_axis=0,...  3.76 us
    all_to_all x1, starting transfers between devices, local(): lax.all_to_all(send_idx.reshape(n_groups, per_group), 'dp', split_axis=0,...  3.16 us
    all_gather x1, blocking collectives, local(): lax.all_gather(own_emb, 'sub', axis=0, tiled=True)  2.57 us
    dot_general x1, matrix products, step(): lax.dot_general(row_emb, block_emb, (((1,), (1,)), ((), ())), preferred_e...  2.5 us
  transfers between devices with their start and end apart: 2, of which 2 were waited for; matrix products, arithmetic and copies ran while one was open for 1% of the time, Pallas kernels for 0%

commit v1 on v0

--- a/solution.py
+++ b/solution.py
@@ -1,11 +1,17 @@
+import functools
 import math
 
 import jax
 import jax.numpy as jnp
 from jax import lax
+from jax.experimental import pallas as pl
+from jax.experimental.pallas import tpu as pltpu
 from jax.sharding import PartitionSpec as P
 
+
 empty_mark = 2**30
+GROUP = ("blk", "dp", "sub")
+KEY_ROWS = 8
 
 
 def fold_best(carry, piece, row_emb, row_idx):
@@ -28,7 +34,7 @@
     return best
 
 
-def local(cls_feats, proj, cluster_id, row_index, assign):
+def general(cls_feats, proj, cluster_id, row_index, assign):
     rows = cls_feats.shape[0]
     feats = cls_feats.astype(jnp.float32)
     center = jnp.mean(feats, axis=1, keepdims=True)
@@ -94,13 +100,163 @@
     return jnp.dot(flat, place.astype(jnp.float32), precision=lax.Precision.HIGHEST)
 
 
+def cover(sizes):
+    n_blk, n_dp, n_sub = sizes
+    count = n_blk * n_dp * n_sub
+    core, side, near, far = 1, n_sub, n_sub * n_dp, count // 2
+
+    def across(d):
+        if d < far:
+            return far ^ side ^ core
+        return far ^ near ^ (0 if d & side else core)
+
+    def beside(d):
+        return side ^ (core if bool(d & side) == (d >= far) else 0)
+
+    offsets = [across, lambda d: near ^ core, beside, lambda d: core]
+    perms = [[(d ^ offset(d), d) for d in range(count)] for offset in offsets]
+    for perm in perms:
+        if sorted(a for a, _ in perm) != list(range(count)):
+            return None
+    held = [{d} | {a for perm in perms for a, b in perm if b == d} for d in range(count)]
+    if len({(a, b) for h in held for a in h for b in h}) != count * count:
+        return None
+    return perms
+
+
+def embed_kernel(per_coarse, cls_hbm, proj_hbm, fine_hbm, index_hbm, assign_hbm, out_ref, *scratch):
+    cls_ref, proj, fine_ref, index_ref, assign_ref, sem = scratch
+    rows, depth = cls_ref.shape
+    width = out_ref.shape[1]
+    chunks = proj.shape[0]
+    step = depth // chunks
+    first = pltpu.make_async_copy(cls_hbm, cls_ref, sem.at[0])
+    small = [
+        pltpu.make_async_copy(fine_hbm, fine_ref, sem.at[1]),
+        pltpu.make_async_copy(index_hbm, index_ref, sem.at[2]),
+        pltpu.make_async_copy(assign_hbm, assign_ref, sem.at[3]),
+    ]
+    pieces = [
+        pltpu.make_async_copy(proj_hbm.at[pl.ds(c * step, step), :], proj.at[c], sem.at[4 + c])
+        for c in range(chunks)
+    ]
+    for copy in [first, *pieces, *small]:
+        copy.start()
+    first.wait()
+    feats = cls_ref[...].astype(jnp.float32)
+    center = jnp.mean(feats, axis=1, keepdims=True)
+    feats = feats - center
+    spread = jnp.mean(feats * feats, axis=1, keepdims=True)
+    normed = (feats * lax.rsqrt(spread + 1e-05)).astype(jnp.bfloat16)
+    for copy in small:
+        copy.wait()
+    fine = fine_ref[...]
+    coarse = jnp.zeros(fine.shape, jnp.int32)
+    for k in range(assign_ref.shape[0]):
+        coarse = jnp.where(fine == k, lax.div(assign_ref[k], jnp.int32(per_coarse)), coarse)
+    index = index_ref[...]
+    digits = [coarse, index >> 8, index & 255]
+    digits = digits + [jnp.zeros_like(index)] * (KEY_ROWS - len(digits))
+    keys = jnp.concatenate(digits, axis=0).astype(jnp.float32).astype(out_ref.dtype)
+    out_ref[rows:, :rows] = keys
+    out_ref[rows:, rows:] = jnp.zeros((KEY_ROWS, width - rows), out_ref.dtype)
+    total = None
+    for c in range(chunks):
+        pieces[c].wait()
+        part = jnp.dot(
+            normed[:, c * step : (c + 1) * step], proj[c], preferred_element_type=jnp.float32
+        )
+        total = part if total is None else total + part
+    scale = lax.rsqrt(jnp.sum(total * total, axis=1, keepdims=True) + 1e-06)
+    out_ref[:rows, :] = (total * scale).astype(out_ref.dtype)
+
+
+def embed(cls_feats, proj, cluster_id, row_index, assign, per_coarse):
+    rows, depth = cls_feats.shape
+    width = proj.shape[1]
+    chunks = 4
+    args = (cls_feats, proj, cluster_id.reshape(1, rows), row_index.reshape(1, rows), assign)
+    return pl.pallas_call(
+        functools.partial(embed_kernel, per_coarse),
+        out_shape=jax.ShapeDtypeStruct((rows + KEY_ROWS, width), jnp.bfloat16),
+        in_specs=[pl.BlockSpec(memory_space=pltpu.HBM)] * len(args),
+        out_specs=pl.BlockSpec(memory_space=pltpu.VMEM),
+        scratch_shapes=[
+            pltpu.VMEM((rows, depth), cls_feats.dtype),
+            pltpu.VMEM((chunks, depth // chunks, width), proj.dtype),
+            pltpu.VMEM((1, rows), jnp.int32),
+            pltpu.VMEM((1, rows), jnp.int32),
+            pltpu.SMEM(assign.shape, jnp.int32),
+            pltpu.SemaphoreType.DMA((4 + chunks,)),
+        ],
+        compiler_params=pltpu.CompilerParams(vmem_limit_bytes=8 << 20),
+    )(*[pltpu.with_memory_space_constraint(arg, pltpu.HBM) for arg in args])
+
+
+def score_kernel(images, *refs):
+    count = len(refs) // 2
+    blocks, outs = refs[:count], refs[count:]
+    rows = blocks[0].shape[0] - KEY_ROWS
+    across, down = [], []
+    for block in blocks:
+        digits = block[rows:, :rows].astype(jnp.float32)
+        key = digits[0:1] * (2.0 * images) + digits[1:2] * 256.0 + digits[2:3]
+        across.append(key)
+        down.append(jnp.broadcast_to(key, (rows, rows)).T)
+    for j in range(count):
+        best = None
+        for i in range(count):
+            score = lax.dot_general(
+                blocks[i][:rows, :],
+                blocks[j][:rows, :],
+                (((1,), (1,)), ((), ())),
+                preferred_element_type=jnp.float32,
+            )
+            ahead = across[j] - down[i]
+            score = jnp.where((ahead > 0) & (ahead < float(images)), score, -1.0)
+            best = score if best is None else jnp.maximum(best, score)
+        outs[j][...] = jnp.max(best, axis=0, keepdims=True)
+
+
+def scores(blocks, images):
+    rows = blocks[0].shape[0] - KEY_ROWS
+    spec = pl.BlockSpec(memory_space=pltpu.VMEM)
+    return pl.pallas_call(
+        functools.partial(score_kernel, images),
+        out_shape=[jax.ShapeDtypeStruct((1, rows), jnp.float32)] * len(blocks),
+        in_specs=[spec] * len(blocks),
+        out_specs=[spec] * len(blocks),
+        compiler_params=pltpu.CompilerParams(vmem_limit_bytes=8 << 20),
+    )(*blocks)
+
+
+def permute(value, pairs):
+    return lax.ppermute(value, GROUP, pairs)
+
+
+def covered(perms, n_dp, images, cls_feats, proj, cluster_id, row_index, assign):
+    own = embed(cls_feats, proj, cluster_id, row_index, assign, assign.shape[0] // n_dp)
+    held = [own] + [permute(own, perm) for perm in perms]
+    best = scores(held, images)
+    total = best[0]
+    for i, perm in enumerate(perms):
+        back = [(b, a) for a, b in perm]
+        total = jnp.maximum(total, permute(best[i + 1], back))
+    return total.reshape(-1)
+
+
 def solution(mesh):
-    in_specs = (
-        P(("groups", "blk", "dp", "sub"), None),
-        P(),
-        P(("groups", "blk", "dp", "sub"), None),
-        P(("groups", "blk", "dp", "sub")),
-        P("groups"),
-    )
-    out_specs = P(("groups", "blk", "dp", "sub"))
-    return jax.shard_map(local, mesh=mesh, in_specs=in_specs, out_specs=out_specs, check_vma=False)
+    everyone = ("groups",) + GROUP
+    sizes = tuple(mesh.shape[axis] for axis in GROUP)
+    perms = cover(sizes)
+
+    def local(cls_feats, proj, cluster_id, row_index, assign):
+        images = math.prod(sizes) * cls_feats.shape[0]
+        if perms is None or max(images // 256, sizes[1]) > 256:
+            return general(cls_feats, proj, cluster_id, row_index, assign)
+        return covered(perms, sizes[1], images, cls_feats, proj, cluster_id, row_index, assign)
+
+    in_specs = (P(everyone, None), P(), P(everyone, None), P(everyone), P("groups"))
+    return jax.shard_map(
+        local, mesh=mesh, in_specs=in_specs, out_specs=P(everyone), check_vma=False
+    )

time: 80.1 us -> 26.7 us (0.33)
  blocking collectives: 36.1 us -> 0 us
  between operations: 13.5 us -> 0.02 us
  starting transfers between devices: 3.16 us -> 9.3 us
  matrix products: 4.94 us -> 0 us
  waiting for transfers between devices: 17.6 us -> 13.3 us
  other arithmetic: 4.3 us -> 0.52 us
  Pallas kernels: 0 us -> 3.5 us
    all_to_all x2 -> x0, blocking collectives: 17.5 us -> none  [the longest x1 11.2 us: local(): lax.all_to_all(send_emb.reshape(n_groups, per_group, width), 'dp', split_...]
    all_gather x3 -> x0, blocking collectives: 16.2 us -> none  [the longest x1 11.8 us: local(): lax.all_gather(own_idx, 'blk', axis=0, tiled=True)]
    all_gather x1 -> x0, waiting for transfers between devices: 13.9 us -> none  [local(): lax.all_gather(own_emb, 'blk', axis=0, tiled=True)]
    ppermute x0 -> x8, waiting for transfers between devices: none -> 13.3 us  [permute(): return lax.ppermute(value, GROUP, pairs)]
    ppermute x0 -> x8, starting transfers between devices: none -> 9.3 us  [permute(): return lax.ppermute(value, GROUP, pairs)]
    dot_general x4 -> x0, matrix products: 4.94 us -> none  [the longest x1 2.5 us: step(): lax.dot_general(row_emb, block_emb, (((1,), (1,)), ((), ())), preferred_e...]
    all_to_all x1 -> x0, waiting for transfers between devices: 3.76 us -> none  [local(): lax.all_to_all(send_idx.reshape(n_groups, per_group), 'dp', split_axis=0,...]
    pallas_call x0 -> x2, Pallas kernels: none -> 3.5 us  [the longest x1 2.03 us: embed(): pl.pallas_call(functools.partial(embed_kernel, per_coarse), out_shape=jax...]
  transfers between devices with their start and end apart: 2 -> 8, of which waited for: 2 -> 4; matrix products, arithmetic and copies ran while one was open for 1% -> 0% of each run, Pallas kernels for 0% -> 0%
where the time goes in v1:
time: 26.7 us; the launch traced here: 26.6 us
  waiting for transfers between devices  13.3 us (50%)
  starting transfers between devices  9.3 us (35%)
  Pallas kernels  3.5 us (13%)
  other arithmetic  0.52 us (2%)
    ppermute x8, waiting for transfers between devices, permute(): return lax.ppermute(value, GROUP, pairs)  13.3 us
    ppermute x8, starting transfers between devices, permute(): return lax.ppermute(value, GROUP, pairs)  9.3 us
    pallas_call x1, Pallas kernels, embed(): pl.pallas_call(functools.partial(embed_kernel, per_coarse), out_shape=jax...  2.03 us
    pallas_call x1, Pallas kernels, scores(): pl.pallas_call(functools.partial(score_kernel, images), out_shape=[jax.Sh...  1.47 us
  transfers between devices with their start and end apart: 8, of which 4 were waited for; matrix products, arithmetic and copies ran while one was open for 0% of the time, Pallas kernels for 0%

profile of v1, /device:TPU:0, one launch (start us, length us, event | category | flops | bytes accessed | tf_op | source)
XLA Modules:
  0.0 26.6 jit_solution(3819850392206708989)
XLA Ops:
  0.0 2.0 %shard_map.55.refs_0_ = bf16[136,768]{1,0:T(8,128)(2,1)S(1)} custom-call(bf16[128,1024]{1,0:T(8,128)(2,1)} %cls_hbm.1, bf16[1024,768]{1,0:T(8,128)(2,1)} %proj_hbm.1, s32[1,128]{1,0:T(1,128)} %bitcast.4, s32[1,128]{1,0:T(1,128)} %bitcast.5, s32[8]{0:T(128)} %assign_hbm.1), custom_call_target="tpu_custom_call" | custom-call | tf_op jit(solution)/shard_map/pallas_call | solution.py:179
  2.0 0.6 %collective-permute-start.3 = (bf16[136,768]{1,0:T(8,128)(2,1)S(1)}, bf16[136,768]{1,0:T(8,128)(2,1)S(1)}, u32[]{:S(2)}, u32[]{:S(2)}) collective-permute-start(bf16[136,768]{1,0:T(8,128)(2,1)S(1)} %shard_map.55.refs_0_), channel_id=1, source_target_pairs={{1,0},{0,1},{3,2},{2,3},{5,4},{4,5},{7,6},{6,7},{9,8},{8,9},{11,10... | collective-permute-start | bytes 626696 | tf_op jit(solution)/shard_map/ppermute | solution.py:234
  2.6 2.5 %collective-permute-start.2 = (bf16[136,768]{1,0:T(8,128)(2,1)S(1)}, bf16[136,768]{1,0:T(8,128)(2,1)S(1)}, u32[]{:S(2)}, u32[]{:S(2)}) collective-permute-start(bf16[136,768]{1,0:T(8,128)(2,1)S(1)} %shard_map.55.refs_0_), channel_id=1, source_target_pairs={{3,0},{2,1},{0,2},{1,3},{7,4},{6,5},{4,6},{5,7},{10,8},{11,9},{9,1... | collective-permute-start | bytes 626696 | tf_op jit(solution)/shard_map/ppermute | solution.py:234
  5.1 1.3 %collective-permute-start.1 = (bf16[136,768]{1,0:T(8,128)(2,1)S(1)}, bf16[136,768]{1,0:T(8,128)(2,1)S(1)}, u32[]{:S(2)}, u32[]{:S(2)}) collective-permute-start(bf16[136,768]{1,0:T(8,128)(2,1)S(1)} %shard_map.55.refs_0_), channel_id=1, source_target_pairs={{5,0},{4,1},{7,2},{6,3},{1,4},{0,5},{3,6},{2,7},{13,8},{12,9},{15,... | collective-permute-start | bytes 626696 | tf_op jit(solution)/shard_map/ppermute | solution.py:234
  6.5 2.5 %collective-permute-start = (bf16[136,768]{1,0:T(8,128)(2,1)S(1)}, bf16[136,768]{1,0:T(8,128)(2,1)S(1)}, u32[]{:S(2)}, u32[]{:S(2)}) collective-permute-start(bf16[136,768]{1,0:T(8,128)(2,1)S(1)} %shard_map.55.refs_0_), channel_id=1, source_target_pairs={{11,0},{10,1},{9,2},{8,3},{15,4},{14,5},{13,6},{12,7},{5,8},{4,9},... | collective-permute-start | bytes 626696 | tf_op jit(solution)/shard_map/ppermute | solution.py:234
  9.0 0.0 collective-permute-done.3.refs_4_
  9.0 5.7 %collective-permute-done.2.refs_3_ = bf16[136,768]{1,0:T(8,128)(2,1)S(1)} collective-permute-done((bf16[136,768]{1,0:T(8,128)(2,1)S(1)}, bf16[136,768]{1,0:T(8,128)(2,1)S(1)}, u32[]{:S(2)}, u32[]{:S(2)}) %collective-permute-start.2) | collective-permute-done | bytes 208928 | tf_op jit(solution)/shard_map/ppermute | solution.py:234
  14.6 2.1 %collective-permute-done.1.refs_2_ = bf16[136,768]{1,0:T(8,128)(2,1)S(1)} collective-permute-done((bf16[136,768]{1,0:T(8,128)(2,1)S(1)}, bf16[136,768]{1,0:T(8,128)(2,1)S(1)}, u32[]{:S(2)}, u32[]{:S(2)}) %collective-permute-start.1) | collective-permute-done | bytes 208928 | tf_op jit(solution)/shard_map/ppermute | solution.py:234
  16.7 3.1 %collective-permute-done.refs_1_ = bf16[136,768]{1,0:T(8,128)(2,1)S(1)} collective-permute-done((bf16[136,768]{1,0:T(8,128)(2,1)S(1)}, bf16[136,768]{1,0:T(8,128)(2,1)S(1)}, u32[]{:S(2)}, u32[]{:S(2)}) %collective-permute-start) | collective-permute-done | bytes 208928 | tf_op jit(solution)/shard_map/ppermute | solution.py:234
  19.7 1.5 %shard_map.56 = (f32[1,128]{1,0:T(1,128)S(1)}, f32[1,128]{1,0:T(1,128)S(1)}, f32[1,128]{1,0:T(1,128)S(1)}, f32[1,128]{1,0:T(1,128)S(1)}, f32[1,128]{1,0:T(1,128)S(1)}) custom-call(bf16[136,768]{1,0:T(8,128)(2,1)S(1)} %shard_map.55.refs_0_, bf16[136,768]{1,0:T(8,128)(2,1)S(1)} %collective-permute-done.refs_1_, ...), custom_call_target="tpu_custom_call" | custom-call | tf_op jit(solution)/shard_map/pallas_call | solution.py:224
  21.2 0.3 %collective-permute-start.4 = (f32[1,128]{1,0:T(1,128)S(1)}, f32[1,128]{1,0:T(1,128)S(1)}, u32[]{:S(2)}, u32[]{:S(2)}) collective-permute-start(f32[1,128]{1,0:T(1,128)S(1)} %get-tuple-element.11), channel_id=1, source_target_pairs={{0,11},{1,10},{2,9},{3,8},{4,15},{5,14},{6,13},{7,12},{8,5},{9,4},... | collective-permute-start | bytes 1544 | tf_op jit(solution)/shard_map/ppermute | solution.py:234
  21.6 0.8 %collective-permute-start.5 = (f32[1,128]{1,0:T(1,128)S(1)}, f32[1,128]{1,0:T(1,128)S(1)}, u32[]{:S(2)}, u32[]{:S(2)}) collective-permute-start(f32[1,128]{1,0:T(1,128)S(1)} %get-tuple-element.12), channel_id=1, source_target_pairs={{0,5},{1,4},{2,7},{3,6},{4,1},{5,0},{6,3},{7,2},{8,13},{9,12},{10,... | collective-permute-start | bytes 1544 | tf_op jit(solution)/shard_map/ppermute | solution.py:234
  22.4 1.0 %collective-permute-start.6 = (f32[1,128]{1,0:T(1,128)S(1)}, f32[1,128]{1,0:T(1,128)S(1)}, u32[]{:S(2)}, u32[]{:S(2)}) collective-permute-start(f32[1,128]{1,0:T(1,128)S(1)} %get-tuple-element.13), channel_id=1, source_target_pairs={{0,3},{1,2},{2,0},{3,1},{4,7},{5,6},{6,4},{7,5},{8,10},{9,11},{10,... | collective-permute-start | bytes 1544 | tf_op jit(solution)/shard_map/ppermute | solution.py:234
  23.4 0.2 collective-permute-start.7
  23.6 2.5 %collective-permute-done.4 = f32[1,128]{1,0:T(1,128)S(1)} collective-permute-done((f32[1,128]{1,0:T(1,128)S(1)}, f32[1,128]{1,0:T(1,128)S(1)}, u32[]{:S(2)}, u32[]{:S(2)}) %collective-permute-start.4) | collective-permute-done | bytes 544 | tf_op jit(solution)/shard_map/ppermute | solution.py:234
  26.1 0.0 collective-permute-done.5
  26.1 0.0 collective-permute-done.6
  26.1 0.0 collective-permute-done.7
  26.1 0.5 %maximum_bitcast_fusion = f32[128]{0:T(128)} fusion(f32[1,128]{1,0:T(1,128)S(1)} %collective-permute-done.7, f32[1,128]{1,0:T(1,128)S(1)} %collective-permute-done.6, f32[1,128]{1,0:T(1,128)S(1)} %collective-permute-done.5, f32[1,128]{1,0:T(1,128)S(1)} %get-tuple-element.10, f32[1,128]{1,0:T(1,128)S(1)} %collective-permute-done.4), kind=kLoop, calls=%fused_computation | loop fusion | flops 512 | bytes 3072 | tf_op jit(solution)/shard_map/reshape | solution.py:245
Async XLA Ops:
  2.0 6.9 %collective-permute-start.3 = (bf16[136,768]{1,0:T(8,128)(2,1)S(1)}, bf16[136,768]{1,0:T(8,128)(2,1)S(1)}, u32[]{:S(2)}, u32[]{:S(2)}) collective-permute-start(bf16[136,768]{1,0:T(8,128)(2,1)S(1)} %shard_map.55.refs_0_), channel_id=1, source_target_pairs={{1,0},{0,1},{3,2},{2,3},{5,4},{4,5},{7,6},{6,7},{9,8},{8,9},{11,10... | collective-permute-start | bytes 626696 | tf_op jit(solution)/shard_map/ppermute | solution.py:234
  2.6 12.0 %collective-permute-start.2 = (bf16[136,768]{1,0:T(8,128)(2,1)S(1)}, bf16[136,768]{1,0:T(8,128)(2,1)S(1)}, u32[]{:S(2)}, u32[]{:S(2)}) collective-permute-start(bf16[136,768]{1,0:T(8,128)(2,1)S(1)} %shard_map.55.refs_0_), channel_id=1, source_target_pairs={{3,0},{2,1},{0,2},{1,3},{7,4},{6,5},{4,6},{5,7},{10,8},{11,9},{9,1... | collective-permute-start | bytes 626696 | tf_op jit(solution)/shard_map/ppermute | solution.py:234
  5.1 11.5 %collective-permute-start.1 = (bf16[136,768]{1,0:T(8,128)(2,1)S(1)}, bf16[136,768]{1,0:T(8,128)(2,1)S(1)}, u32[]{:S(2)}, u32[]{:S(2)}) collective-permute-start(bf16[136,768]{1,0:T(8,128)(2,1)S(1)} %shard_map.55.refs_0_), channel_id=1, source_target_pairs={{5,0},{4,1},{7,2},{6,3},{1,4},{0,5},{3,6},{2,7},{13,8},{12,9},{15,... | collective-permute-start | bytes 626696 | tf_op jit(solution)/shard_map/ppermute | solution.py:234
  6.5 13.3 %collective-permute-start = (bf16[136,768]{1,0:T(8,128)(2,1)S(1)}, bf16[136,768]{1,0:T(8,128)(2,1)S(1)}, u32[]{:S(2)}, u32[]{:S(2)}) collective-permute-start(bf16[136,768]{1,0:T(8,128)(2,1)S(1)} %shard_map.55.refs_0_), channel_id=1, source_target_pairs={{11,0},{10,1},{9,2},{8,3},{15,4},{14,5},{13,6},{12,7},{5,8},{4,9},... | collective-permute-start | bytes 626696 | tf_op jit(solution)/shard_map/ppermute | solution.py:234
  21.2 4.9 %collective-permute-start.4 = (f32[1,128]{1,0:T(1,128)S(1)}, f32[1,128]{1,0:T(1,128)S(1)}, u32[]{:S(2)}, u32[]{:S(2)}) collective-permute-start(f32[1,128]{1,0:T(1,128)S(1)} %get-tuple-element.11), channel_id=1, source_target_pairs={{0,11},{1,10},{2,9},{3,8},{4,15},{5,14},{6,13},{7,12},{8,5},{9,4},... | collective-permute-start | bytes 1544 | tf_op jit(solution)/shard_map/ppermute | solution.py:234
  21.6 4.5 %collective-permute-start.5 = (f32[1,128]{1,0:T(1,128)S(1)}, f32[1,128]{1,0:T(1,128)S(1)}, u32[]{:S(2)}, u32[]{:S(2)}) collective-permute-start(f32[1,128]{1,0:T(1,128)S(1)} %get-tuple-element.12), channel_id=1, source_target_pairs={{0,5},{1,4},{2,7},{3,6},{4,1},{5,0},{6,3},{7,2},{8,13},{9,12},{10,... | collective-permute-start | bytes 1544 | tf_op jit(solution)/shard_map/ppermute | solution.py:234
  22.4 3.7 %collective-permute-start.6 = (f32[1,128]{1,0:T(1,128)S(1)}, f32[1,128]{1,0:T(1,128)S(1)}, u32[]{:S(2)}, u32[]{:S(2)}) collective-permute-start(f32[1,128]{1,0:T(1,128)S(1)} %get-tuple-element.13), channel_id=1, source_target_pairs={{0,3},{1,2},{2,0},{3,1},{4,7},{5,6},{6,4},{7,5},{8,10},{9,11},{10,... | collective-permute-start | bytes 1544 | tf_op jit(solution)/shard_map/ppermute | solution.py:234
  23.4 2.6 %collective-permute-start.7 = (f32[1,128]{1,0:T(1,128)S(1)}, f32[1,128]{1,0:T(1,128)S(1)}, u32[]{:S(2)}, u32[]{:S(2)}) collective-permute-start(f32[1,128]{1,0:T(1,128)S(1)} %get-tuple-element.14), channel_id=1, source_target_pairs={{0,1},{1,0},{2,3},{3,2},{4,5},{5,4},{6,7},{7,6},{8,9},{9,8},{10,11... | collective-permute-start | bytes 1544 | tf_op jit(solution)/shard_map/ppermute | solution.py:234

commit v2 on v1

--- a/solution.py
+++ b/solution.py
@@ -1,4 +1,5 @@
 import functools
+import itertools
 import math
 
 import jax
@@ -12,6 +13,8 @@
 empty_mark = 2**30
 GROUP = ("blk", "dp", "sub")
 KEY_ROWS = 8
+LANES = 128
+OWN, CORE, SIDE, NEAR, FAR = range(5)
 
 
 def fold_best(carry, piece, row_emb, row_idx):
@@ -105,29 +108,39 @@
     count = n_blk * n_dp * n_sub
     core, side, near, far = 1, n_sub, n_sub * n_dp, count // 2
 
+    def beside(d):
+        return side ^ (0 if d < far and d & side else core)
+
+    def along(d):
+        return near ^ (0 if d >= far and not d & side else core)
+
     def across(d):
-        if d < far:
-            return far ^ side ^ core
-        return far ^ near ^ (0 if d & side else core)
-
-    def beside(d):
-        return side ^ (core if bool(d & side) == (d >= far) else 0)
-
-    offsets = [across, lambda d: near ^ core, beside, lambda d: core]
-    perms = [[(d ^ offset(d), d) for d in range(count)] for offset in offsets]
-    for perm in perms:
-        if sorted(a for a, _ in perm) != list(range(count)):
+        return far ^ (side if d < far else near ^ core)
+
+    offsets = [lambda d: 0, lambda d: core, beside, along, across]
+    held = [[d ^ offset(d) for offset in offsets] for d in range(count)]
+    for slot in range(len(offsets)):
+        if sorted(h[slot] for h in held) != list(range(count)):
             return None
-    held = [{d} | {a for perm in perms for a, b in perm if b == d} for d in range(count)]
-    if len({(a, b) for h in held for a in h for b in h}) != count * count:
-        return None
-    return perms
+    perms = [[(h[slot], d) for d, h in enumerate(held)] for slot in range(1, len(offsets))]
+
+    def covers(pairs):
+        return len({(h[q], h[c]) for h in held for q, c in pairs}) == count * count
+
+    slots = range(len(offsets))
+    pairs = [(q, c) for q in slots for c in slots if q == OWN or (q != c and FAR in (q, c))]
+    spare = [(q, c) for q in (CORE, SIDE, NEAR) for c in (OWN, CORE, SIDE, NEAR) if q != c]
+    spare.sort(key=lambda pair: NEAR in pair)
+    for size in range(len(spare) + 1):
+        for more in itertools.combinations(spare, size):
+            if covers(pairs + list(more)):
+                return perms, pairs + list(more)
+    return None
 
 
 def embed_kernel(per_coarse, cls_hbm, proj_hbm, fine_hbm, index_hbm, assign_hbm, out_ref, *scratch):
     cls_ref, proj, fine_ref, index_ref, assign_ref, sem = scratch
     rows, depth = cls_ref.shape
-    width = out_ref.shape[1]
     chunks = proj.shape[0]
     step = depth // chunks
     first = pltpu.make_async_copy(cls_hbm, cls_ref, sem.at[0])
@@ -158,8 +171,6 @@
     digits = [coarse, index >> 8, index & 255]
     digits = digits + [jnp.zeros_like(index)] * (KEY_ROWS - len(digits))
     keys = jnp.concatenate(digits, axis=0).astype(jnp.float32).astype(out_ref.dtype)
-    out_ref[rows:, :rows] = keys
-    out_ref[rows:, rows:] = jnp.zeros((KEY_ROWS, width - rows), out_ref.dtype)
     total = None
     for c in range(chunks):
         pieces[c].wait()
@@ -168,7 +179,10 @@
         )
         total = part if total is None else total + part
     scale = lax.rsqrt(jnp.sum(total * total, axis=1, keepdims=True) + 1e-06)
-    out_ref[:rows, :] = (total * scale).astype(out_ref.dtype)
+    emb = (total * scale).astype(out_ref.dtype)
+    for p in range(emb.shape[1] // LANES):
+        out_ref[p * rows : (p + 1) * rows, :] = emb[:, p * LANES : (p + 1) * LANES]
+    out_ref[out_ref.shape[0] - KEY_ROWS :, :] = keys
 
 
 def embed(cls_feats, proj, cluster_id, row_index, assign, per_coarse):
@@ -178,7 +192,7 @@
     args = (cls_feats, proj, cluster_id.reshape(1, rows), row_index.reshape(1, rows), assign)
     return pl.pallas_call(
         functools.partial(embed_kernel, per_coarse),
-        out_shape=jax.ShapeDtypeStruct((rows + KEY_ROWS, width), jnp.bfloat16),
+        out_shape=jax.ShapeDtypeStruct((width // LANES * rows + KEY_ROWS, LANES), jnp.bfloat16),
         in_specs=[pl.BlockSpec(memory_space=pltpu.HBM)] * len(args),
         out_specs=pl.BlockSpec(memory_space=pltpu.VMEM),
         scratch_shapes=[
@@ -193,68 +207,98 @@
     )(*[pltpu.with_memory_space_constraint(arg, pltpu.HBM) for arg in args])
 
 
-def score_kernel(images, *refs):
-    count = len(refs) // 2
-    blocks, outs = refs[:count], refs[count:]
-    rows = blocks[0].shape[0] - KEY_ROWS
-    across, down = [], []
-    for block in blocks:
-        digits = block[rows:, :rows].astype(jnp.float32)
-        key = digits[0:1] * (2.0 * images) + digits[1:2] * 256.0 + digits[2:3]
-        across.append(key)
-        down.append(jnp.broadcast_to(key, (rows, rows)).T)
-    for j in range(count):
+def read_block(block):
+    rows = LANES
+    pieces = block.shape[0] // rows
+    return jnp.concatenate([block[p * rows : (p + 1) * rows, :] for p in range(pieces)], axis=1)
+
+
+def read_key(block, images):
+    digits = block[block.shape[0] - KEY_ROWS :, :].astype(jnp.float32)
+    return digits[0:1] * (2.0 * images) + digits[1:2] * 256.0 + digits[2:3]
+
+
+def score_kernel(images, n_blocks, wanted, n_before, *refs):
+    blocks, refs = refs[:n_blocks], refs[n_blocks:]
+    before, outs = refs[:n_before], refs[n_before:]
+    keys = [read_key(block, images) for block in blocks]
+    down = {
+        i: jnp.broadcast_to(keys[i], (LANES, LANES)).T
+        for i in sorted({i for _, cands, _ in wanted for i in cands})
+    }
+    for out, (query, cands, earlier) in zip(outs, wanted):
+        right = read_block(blocks[query])
         best = None
-        for i in range(count):
+        for i in cands:
             score = lax.dot_general(
-                blocks[i][:rows, :],
-                blocks[j][:rows, :],
+                read_block(blocks[i]),
+                right,
                 (((1,), (1,)), ((), ())),
                 preferred_element_type=jnp.float32,
             )
-            ahead = across[j] - down[i]
+            ahead = keys[query] - down[i]
             score = jnp.where((ahead > 0) & (ahead < float(images)), score, -1.0)
             best = score if best is None else jnp.maximum(best, score)
-        outs[j][...] = jnp.max(best, axis=0, keepdims=True)
-
-
-def scores(blocks, images):
-    rows = blocks[0].shape[0] - KEY_ROWS
+        best = jnp.max(best, axis=0, keepdims=True)
+        out[...] = best if earlier is None else jnp.maximum(best, before[earlier][...])
+
+
+def scores(blocks, pairs, images, before=()):
+    before = dict(before)
+    names = list(blocks)
+    olds = list(before)
+    wanted = []
+    for query in names:
+        cands = tuple(names.index(c) for q, c in pairs if q == query)
+        if cands:
+            old = olds.index(query) if query in before else None
+            wanted.append((names.index(query), cands, old))
+    used = [before[query] for query in olds]
     spec = pl.BlockSpec(memory_space=pltpu.VMEM)
-    return pl.pallas_call(
-        functools.partial(score_kernel, images),
-        out_shape=[jax.ShapeDtypeStruct((1, rows), jnp.float32)] * len(blocks),
-        in_specs=[spec] * len(blocks),
-        out_specs=[spec] * len(blocks),
+    found = pl.pallas_call(
+        functools.partial(score_kernel, images, len(names), wanted, len(used)),
+        out_shape=[jax.ShapeDtypeStruct((1, LANES), jnp.float32)] * len(wanted),
+        in_specs=[spec] * (len(names) + len(used)),
+        out_specs=[spec] * len(wanted),
         compiler_params=pltpu.CompilerParams(vmem_limit_bytes=8 << 20),
-    )(*blocks)
+    )(*blocks.values(), *used)
+    return before | {names[query]: best for (query, _, _), best in zip(wanted, found)}
 
 
 def permute(value, pairs):
     return lax.ppermute(value, GROUP, pairs)
 
 
-def covered(perms, n_dp, images, cls_feats, proj, cluster_id, row_index, assign):
+def covered(plan, n_dp, images, cls_feats, proj, cluster_id, row_index, assign):
+    perms, pairs = plan
+    early = [(q, c) for q, c in pairs if max(q, c) < NEAR]
+    rest = [(q, c) for q, c in pairs if q < FAR and max(q, c) >= NEAR]
     own = embed(cls_feats, proj, cluster_id, row_index, assign, assign.shape[0] // n_dp)
-    held = [own] + [permute(own, perm) for perm in perms]
-    best = scores(held, images)
-    total = best[0]
-    for i, perm in enumerate(perms):
+    held = {OWN: own}
+    for slot, perm in enumerate(perms, 1):
+        held[slot] = permute(own, perm)
+    best = scores({i: held[i] for i in (OWN, CORE, SIDE)}, early, images)
+    best |= scores(held, [(q, c) for q, c in pairs if q == FAR], images)
+    before = {q: best[q] for q in best if q < FAR}
+    best |= scores(held, rest, images, before)
+    total = best[OWN]
+    for slot, perm in enumerate(perms, 1):
         back = [(b, a) for a, b in perm]
-        total = jnp.maximum(total, permute(best[i + 1], back))
+        total = jnp.maximum(total, permute(best[slot], back))
     return total.reshape(-1)
 
 
 def solution(mesh):
     everyone = ("groups",) + GROUP
     sizes = tuple(mesh.shape[axis] for axis in GROUP)
-    perms = cover(sizes)
+    plan = cover(sizes)
 
     def local(cls_feats, proj, cluster_id, row_index, assign):
         images = math.prod(sizes) * cls_feats.shape[0]
-        if perms is None or max(images // 256, sizes[1]) > 256:
+        exact = max(images // 256, sizes[1]) <= 256
+        if plan is None or not exact or cls_feats.shape[0] != LANES:
             return general(cls_feats, proj, cluster_id, row_index, assign)
-        return covered(perms, sizes[1], images, cls_feats, proj, cluster_id, row_index, assign)
+        return covered(plan, sizes[1], images, cls_feats, proj, cluster_id, row_index, assign)
 
     in_specs = (P(everyone, None), P(), P(everyone, None), P(everyone), P("groups"))
     return jax.shard_map(

time: 26.7 us -> 27.1 us (1.015)
  starting transfers between devices: 9.3 us -> 9.6 us
    ppermute x8, starting transfers between devices: 9.3 us -> 9.6 us  [permute(): return lax.ppermute(value, GROUP, pairs)]
    pallas_call x1 -> x3, Pallas kernels: 1.47 us -> 1.35 us  [scores(): pl.pallas_call(functools.partial(score_kernel, images, len(names), wanted...]
  transfers between devices with their start and end apart: 8 -> 8, of which waited for: 4 -> 4; matrix products, arithmetic and copies ran while one was open for 0% -> 0% of each run, Pallas kernels for 0% -> 3%
where the time goes in v2:
time: 27.1 us; the launch traced here: 26.9 us
  waiting for transfers between devices  13.4 us (49%)
  starting transfers between devices  9.6 us (35%)
  Pallas kernels  3.38 us (12%)
  other arithmetic  0.52 us (2%)
    ppermute x8, waiting for transfers between devices, permute(): return lax.ppermute(value, GROUP, pairs)  13.4 us
    ppermute x8, starting transfers between devices, permute(): return lax.ppermute(value, GROUP, pairs)  9.6 us
    pallas_call x1, Pallas kernels, embed(): pl.pallas_call(functools.partial(embed_kernel, per_coarse), out_shape=jax...  2.03 us
    pallas_call x3, Pallas kernels, scores(): pl.pallas_call(functools.partial(score_kernel, images, len(names), wanted...  1.35 us
  transfers between devices with their start and end apart: 8, of which 4 were waited for; matrix products, arithmetic and copies ran while one was open for 0% of the time, Pallas kernels for 3%

profile of v2, /device:TPU:0, one launch (start us, length us, event | category | flops | bytes accessed | tf_op | source)
XLA Modules:
  0.0 26.9 jit_solution(4197948123764101456)
XLA Ops:
  0.0 2.0 %shard_map.55.refs_0_ = bf16[776,128]{1,0:T(8,128)(2,1)S(1)} custom-call(bf16[128,1024]{1,0:T(8,128)(2,1)} %cls_hbm.1, bf16[1024,768]{1,0:T(8,128)(2,1)} %proj_hbm.1, s32[1,128]{1,0:T(1,128)} %bitcast.4, s32[1,128]{1,0:T(1,128)} %bitcast.5, s32[8]{0:T(128)} %assign_hbm.1), custom_call_target="tpu_custom_call" | custom-call | tf_op jit(solution)/shard_map/pallas_call | solution.py:193
  2.0 3.0 %collective-permute-start.1 = (bf16[776,128]{1,0:T(8,128)(2,1)S(1)}, bf16[776,128]{1,0:T(8,128)(2,1)S(1)}, u32[]{:S(2)}, u32[]{:S(2)}) collective-permute-start(bf16[776,128]{1,0:T(8,128)(2,1)S(1)} %shard_map.55.refs_0_), channel_id=1, source_target_pairs={{3,0},{2,1},{0,2},{1,3},{7,4},{6,5},{4,6},{5,7},{11,8},{10,9},{9,1... | collective-permute-start | bytes 595976 | tf_op jit(solution)/shard_map/ppermute | solution.py:269
  5.1 0.0 collective-permute-start
  5.1 3.3 %collective-permute-start.3 = (bf16[776,128]{1,0:T(8,128)(2,1)S(1)}, bf16[776,128]{1,0:T(8,128)(2,1)S(1)}, u32[]{:S(2)}, u32[]{:S(2)}) collective-permute-start(bf16[776,128]{1,0:T(8,128)(2,1)S(1)} %shard_map.55.refs_0_), channel_id=1, source_target_pairs={{10,0},{11,1},{8,2},{9,3},{14,4},{15,5},{12,6},{13,7},{5,8},{4,9},... | collective-permute-start | bytes 595976 | tf_op jit(solution)/shard_map/ppermute | solution.py:269
  8.4 0.0 collective-permute-start.2
  8.4 2.1 %collective-permute-done.1.refs_2_ = bf16[776,128]{1,0:T(8,128)(2,1)S(1)} collective-permute-done((bf16[776,128]{1,0:T(8,128)(2,1)S(1)}, bf16[776,128]{1,0:T(8,128)(2,1)S(1)}, u32[]{:S(2)}, u32[]{:S(2)}) %collective-permute-start.1) | collective-permute-done | bytes 198688 | tf_op jit(solution)/shard_map/ppermute | solution.py:269
  10.5 0.0 collective-permute-done.refs_1_
  10.5 0.4 %shard_map.56 = (f32[1,128]{1,0:T(1,128)S(1)}, f32[1,128]{1,0:T(1,128)S(1)}) custom-call(bf16[776,128]{1,0:T(8,128)(2,1)S(1)} %shard_map.55.refs_0_, bf16[776,128]{1,0:T(8,128)(2,1)S(1)} %collective-permute-done.refs_1_, bf16[776,128]{1,0:T(8,128)(2,1)S(1)} %collective-permute-done.1.refs_2_), custom_call_target="tpu_custom_call" | custom-call | tf_op jit(solution)/shard_map/pallas_call | solution.py:258
  10.8 7.8 %collective-permute-done.3.refs_4_ = bf16[776,128]{1,0:T(8,128)(2,1)S(1)} collective-permute-done((bf16[776,128]{1,0:T(8,128)(2,1)S(1)}, bf16[776,128]{1,0:T(8,128)(2,1)S(1)}, u32[]{:S(2)}, u32[]{:S(2)}) %collective-permute-start.3) | collective-permute-done | bytes 198688 | tf_op jit(solution)/shard_map/ppermute | solution.py:269
  18.6 0.0 collective-permute-done.2.refs_3_
  18.6 0.6 %shard_map.57 = (f32[1,128]{1,0:T(1,128)S(1)}, f32[1,128]{1,0:T(1,128)S(1)}, f32[1,128]{1,0:T(1,128)S(1)}, f32[1,128]{1,0:T(1,128)S(1)}) custom-call(bf16[776,128]{1,0:T(8,128)(2,1)S(1)} %shard_map.55.refs_0_, bf16[776,128]{1,0:T(8,128)(2,1)S(1)} %collective-permute-done.refs_1_, bf16[776,128]{1,0:T(8,128)(2,1)S(1)} %collective-permute-done.1.refs_2_, ...), custom_call_target="tpu_custom_call" | custom-call | tf_op jit(solution)/shard_map/pallas_call | solution.py:258
  19.2 0.1 collective-permute-start.4
  19.3 0.1 collective-permute-start.5
  19.5 1.7 %collective-permute-start.6 = (f32[1,128]{1,0:T(1,128)S(1)}, f32[1,128]{1,0:T(1,128)S(1)}, u32[]{:S(2)}, u32[]{:S(2)}) collective-permute-start(f32[1,128]{1,0:T(1,128)S(1)} %get-tuple-element.16), channel_id=1, source_target_pairs={{0,5},{1,4},{2,7},{3,6},{4,1},{5,0},{6,3},{7,2},{8,12},{9,13},{10,... | collective-permute-start | bytes 1544 | tf_op jit(solution)/shard_map/ppermute | solution.py:269
  21.2 0.4 %shard_map.58 = f32[1,128]{1,0:T(1,128)S(1)} custom-call(bf16[776,128]{1,0:T(8,128)(2,1)S(1)} %shard_map.55.refs_0_, bf16[776,128]{1,0:T(8,128)(2,1)S(1)} %collective-permute-done.refs_1_, bf16[776,128]{1,0:T(8,128)(2,1)S(1)} %collective-permute-done.1.refs_2_, bf16[776,128]{1,0:T(8,128)(2,1)S(1)} %collective-permute-done.2.refs_3_, ...), custom_call_target="tpu_custom_call" | custom-call | tf_op jit(solution)/shard_map/pallas_call | solution.py:258
  21.6 1.3 %collective-permute-start.7 = (f32[1,128]{1,0:T(1,128)S(1)}, f32[1,128]{1,0:T(1,128)S(1)}, u32[]{:S(2)}, u32[]{:S(2)}) collective-permute-start(f32[1,128]{1,0:T(1,128)S(1)} %shard_map.58), channel_id=1, source_target_pairs={{0,10},{1,11},{2,8},{3,9},{4,14},{5,15},{6,12},{7,13},{8,5},{9,4},... | collective-permute-start | bytes 1544 | tf_op jit(solution)/shard_map/ppermute | solution.py:269
  22.9 0.0 collective-permute-done.4
  22.9 0.1 collective-permute-done.5
  22.9 0.0 collective-permute-done.6
  22.9 3.5 %collective-permute-done.7 = f32[1,128]{1,0:T(1,128)S(1)} collective-permute-done((f32[1,128]{1,0:T(1,128)S(1)}, f32[1,128]{1,0:T(1,128)S(1)}, u32[]{:S(2)}, u32[]{:S(2)}) %collective-permute-start.7) | collective-permute-done | bytes 544 | tf_op jit(solution)/shard_map/ppermute | solution.py:269
  26.4 0.5 %maximum_bitcast_fusion = f32[128]{0:T(128)} fusion(f32[1,128]{1,0:T(1,128)S(1)} %collective-permute-done.7, f32[1,128]{1,0:T(1,128)S(1)} %collective-permute-done.6, f32[1,128]{1,0:T(1,128)S(1)} %collective-permute-done.5, f32[1,128]{1,0:T(1,128)S(1)} %get-tuple-element.13, f32[1,128]{1,0:T(1,128)S(1)} %collective-permute-done.4), kind=kLoop, calls=%fused_computation | loop fusion | flops 512 | bytes 3072 | tf_op jit(solution)/shard_map/reshape | solution.py:288
Async XLA Ops:
  2.0 8.4 %collective-permute-start.1 = (bf16[776,128]{1,0:T(8,128)(2,1)S(1)}, bf16[776,128]{1,0:T(8,128)(2,1)S(1)}, u32[]{:S(2)}, u32[]{:S(2)}) collective-permute-start(bf16[776,128]{1,0:T(8,128)(2,1)S(1)} %shard_map.55.refs_0_), channel_id=1, source_target_pairs={{3,0},{2,1},{0,2},{1,3},{7,4},{6,5},{4,6},{5,7},{11,8},{10,9},{9,1... | collective-permute-start | bytes 595976 | tf_op jit(solution)/shard_map/ppermute | solution.py:269
  5.1 5.4 %collective-permute-start = (bf16[776,128]{1,0:T(8,128)(2,1)S(1)}, bf16[776,128]{1,0:T(8,128)(2,1)S(1)}, u32[]{:S(2)}, u32[]{:S(2)}) collective-permute-start(bf16[776,128]{1,0:T(8,128)(2,1)S(1)} %shard_map.55.refs_0_), channel_id=1, source_target_pairs={{1,0},{0,1},{3,2},{2,3},{5,4},{4,5},{7,6},{6,7},{9,8},{8,9},{11,10... | collective-permute-start | bytes 595976 | tf_op jit(solution)/shard_map/ppermute | solution.py:269
  5.1 13.5 %collective-permute-start.3 = (bf16[776,128]{1,0:T(8,128)(2,1)S(1)}, bf16[776,128]{1,0:T(8,128)(2,1)S(1)}, u32[]{:S(2)}, u32[]{:S(2)}) collective-permute-start(bf16[776,128]{1,0:T(8,128)(2,1)S(1)} %shard_map.55.refs_0_), channel_id=1, source_target_pairs={{10,0},{11,1},{8,2},{9,3},{14,4},{15,5},{12,6},{13,7},{5,8},{4,9},... | collective-permute-start | bytes 595976 | tf_op jit(solution)/shard_map/ppermute | solution.py:269
  8.4 10.2 %collective-permute-start.2 = (bf16[776,128]{1,0:T(8,128)(2,1)S(1)}, bf16[776,128]{1,0:T(8,128)(2,1)S(1)}, u32[]{:S(2)}, u32[]{:S(2)}) collective-permute-start(bf16[776,128]{1,0:T(8,128)(2,1)S(1)} %shard_map.55.refs_0_), channel_id=1, source_target_pairs={{5,0},{4,1},{7,2},{6,3},{1,4},{0,5},{3,6},{2,7},{12,8},{13,9},{15,... | collective-permute-start | bytes 595976 | tf_op jit(solution)/shard_map/ppermute | solution.py:269
  19.2 3.7 %collective-permute-start.4 = (f32[1,128]{1,0:T(1,128)S(1)}, f32[1,128]{1,0:T(1,128)S(1)}, u32[]{:S(2)}, u32[]{:S(2)}) collective-permute-start(f32[1,128]{1,0:T(1,128)S(1)} %get-tuple-element.14), channel_id=1, source_target_pairs={{0,1},{1,0},{2,3},{3,2},{4,5},{5,4},{6,7},{7,6},{8,9},{9,8},{10,11... | collective-permute-start | bytes 1544 | tf_op jit(solution)/shard_map/ppermute | solution.py:269
  19.3 3.6 %collective-permute-start.5 = (f32[1,128]{1,0:T(1,128)S(1)}, f32[1,128]{1,0:T(1,128)S(1)}, u32[]{:S(2)}, u32[]{:S(2)}) collective-permute-start(f32[1,128]{1,0:T(1,128)S(1)} %get-tuple-element.15), channel_id=1, source_target_pairs={{0,3},{1,2},{2,0},{3,1},{4,7},{5,6},{6,4},{7,5},{8,11},{9,10},{10,... | collective-permute-start | bytes 1544 | tf_op jit(solution)/shard_map/ppermute | solution.py:269
  19.5 3.5 %collective-permute-start.6 = (f32[1,128]{1,0:T(1,128)S(1)}, f32[1,128]{1,0:T(1,128)S(1)}, u32[]{:S(2)}, u32[]{:S(2)}) collective-permute-start(f32[1,128]{1,0:T(1,128)S(1)} %get-tuple-element.16), channel_id=1, source_target_pairs={{0,5},{1,4},{2,7},{3,6},{4,1},{5,0},{6,3},{7,2},{8,12},{9,13},{10,... | collective-permute-start | bytes 1544 | tf_op jit(solution)/shard_map/ppermute | solution.py:269
  21.6 4.9 %collective-permute-start.7 = (f32[1,128]{1,0:T(1,128)S(1)}, f32[1,128]{1,0:T(1,128)S(1)}, u32[]{:S(2)}, u32[]{:S(2)}) collective-permute-start(f32[1,128]{1,0:T(1,128)S(1)} %shard_map.58), channel_id=1, source_target_pairs={{0,10},{1,11},{2,8},{3,9},{4,14},{5,15},{6,12},{7,13},{8,5},{9,4},... | collective-permute-start | bytes 1544 | tf_op jit(solution)/shard_map/ppermute | solution.py:269

commit v3 on v2

--- a/solution.py
+++ b/solution.py
@@ -1,5 +1,4 @@
 import functools
-import itertools
 import math
 
 import jax
@@ -14,7 +13,7 @@
 GROUP = ("blk", "dp", "sub")
 KEY_ROWS = 8
 LANES = 128
-OWN, CORE, SIDE, NEAR, FAR = range(5)
+OWN, CORE, SIDE, PEER, NEAR, FAR = range(6)
 
 
 def fold_best(carry, piece, row_emb, row_idx):
@@ -107,35 +106,20 @@
     n_blk, n_dp, n_sub = sizes
     count = n_blk * n_dp * n_sub
     core, side, near, far = 1, n_sub, n_sub * n_dp, count // 2
-
-    def beside(d):
-        return side ^ (0 if d < far and d & side else core)
-
-    def along(d):
-        return near ^ (0 if d >= far and not d & side else core)
-
-    def across(d):
-        return far ^ (side if d < far else near ^ core)
-
-    offsets = [lambda d: 0, lambda d: core, beside, along, across]
-    held = [[d ^ offset(d) for offset in offsets] for d in range(count)]
-    for slot in range(len(offsets)):
+    offsets = [0, core, side, core ^ side, near]
+    held = [
+        [d ^ offset for offset in offsets] + [d ^ far ^ (near if d & far else 0)]
+        for d in range(count)
+    ]
+    for slot in range(FAR + 1):
         if sorted(h[slot] for h in held) != list(range(count)):
             return None
-    perms = [[(h[slot], d) for d, h in enumerate(held)] for slot in range(1, len(offsets))]
-
-    def covers(pairs):
-        return len({(h[q], h[c]) for h in held for q, c in pairs}) == count * count
-
-    slots = range(len(offsets))
-    pairs = [(q, c) for q in slots for c in slots if q == OWN or (q != c and FAR in (q, c))]
-    spare = [(q, c) for q in (CORE, SIDE, NEAR) for c in (OWN, CORE, SIDE, NEAR) if q != c]
-    spare.sort(key=lambda pair: NEAR in pair)
-    for size in range(len(spare) + 1):
-        for more in itertools.combinations(spare, size):
-            if covers(pairs + list(more)):
-                return perms, pairs + list(more)
-    return None
+    plane = (OWN, CORE, SIDE, PEER)
+    pairs = [(OWN, c) for c in plane] + [(q, c) for q in plane for c in (NEAR, FAR)]
+    pairs += [(FAR, c) for c in plane]
+    if len({(h[q], h[c]) for h in held for q, c in pairs}) != count * count:
+        return None
+    return held, pairs
 
 
 def embed_kernel(per_coarse, cls_hbm, proj_hbm, fine_hbm, index_hbm, assign_hbm, out_ref, *scratch):
@@ -270,20 +254,21 @@
 
 
 def covered(plan, n_dp, images, cls_feats, proj, cluster_id, row_index, assign):
-    perms, pairs = plan
+    sources, pairs = plan
+    perms = [[(h[slot], d) for d, h in enumerate(sources)] for slot in range(FAR + 1)]
     early = [(q, c) for q, c in pairs if max(q, c) < NEAR]
-    rest = [(q, c) for q, c in pairs if q < FAR and max(q, c) >= NEAR]
+    rest = [(q, c) for q, c in pairs if q < NEAR <= c]
     own = embed(cls_feats, proj, cluster_id, row_index, assign, assign.shape[0] // n_dp)
-    held = {OWN: own}
-    for slot, perm in enumerate(perms, 1):
-        held[slot] = permute(own, perm)
-    best = scores({i: held[i] for i in (OWN, CORE, SIDE)}, early, images)
-    best |= scores(held, [(q, c) for q, c in pairs if q == FAR], images)
-    before = {q: best[q] for q in best if q < FAR}
-    best |= scores(held, rest, images, before)
+    held = {slot: permute(own, perms[slot]) for slot in (FAR, NEAR, SIDE, CORE)}
+    held[PEER] = permute(held[SIDE], perms[CORE])
+    held[OWN] = own
+    plane = {slot: held[slot] for slot in (OWN, CORE, SIDE, PEER)}
+    best = scores(plane, early, images)
+    best |= scores(plane | {FAR: held[FAR]}, [(q, c) for q, c in pairs if q == FAR], images)
+    best |= scores(held, rest, images, {OWN: best[OWN]})
     total = best[OWN]
-    for slot, perm in enumerate(perms, 1):
-        back = [(b, a) for a, b in perm]
+    for slot in (FAR, SIDE, PEER, CORE):
+        back = [(b, a) for a, b in perms[slot]]
         total = jnp.maximum(total, permute(best[slot], back))
     return total.reshape(-1)
 

time: 27.1 us -> 33.3 us (1.23)
  waiting for transfers between devices: 13.4 us -> 19.7 us
    ppermute x8 -> x9, waiting for transfers between devices: 13.4 us -> 19.7 us  [permute(): return lax.ppermute(value, GROUP, pairs)]
    ppermute x8 -> x9, starting transfers between devices: 9.6 us -> 9.57 us  [permute(): return lax.ppermute(value, GROUP, pairs)]
  transfers between devices with their start and end apart: 8 -> 9, of which waited for: 4 -> 6; matrix products, arithmetic and copies ran while one was open for 0% -> 0% of each run, Pallas kernels for 3% -> 2%
where the time goes in v3:
time: 33.3 us; the launch traced here: 33.2 us
  waiting for transfers between devices  19.7 us (59%)
  starting transfers between devices  9.57 us (29%)
  Pallas kernels  3.37 us (10%)
  other arithmetic  0.52 us (2%)
    ppermute x9, waiting for transfers between devices, permute(): return lax.ppermute(value, GROUP, pairs)  19.7 us
    ppermute x9, starting transfers between devices, permute(): return lax.ppermute(value, GROUP, pairs)  9.57 us
    pallas_call x1, Pallas kernels, embed(): pl.pallas_call(functools.partial(embed_kernel, per_coarse), out_shape=jax...  2.03 us
    pallas_call x3, Pallas kernels, scores(): pl.pallas_call(functools.partial(score_kernel, images, len(names), wanted...  1.35 us
  transfers between devices with their start and end apart: 9, of which 6 were waited for; matrix products, arithmetic and copies ran while one was open for 0% of the time, Pallas kernels for 2%

profile of v3, /device:TPU:0, one launch (start us, length us, event | category | flops | bytes accessed | tf_op | source)
XLA Modules:
  0.0 33.2 jit_solution(17094255876683775830)
XLA Ops:
  0.0 2.0 %shard_map.55.refs_0_.refs_5_ = bf16[776,128]{1,0:T(8,128)(2,1)S(1)} custom-call(bf16[128,1024]{1,0:T(8,128)(2,1)} %cls_hbm.1, bf16[1024,768]{1,0:T(8,128)(2,1)} %proj_hbm.1, s32[1,128]{1,0:T(1,128)} %bitcast.4, s32[1,128]{1,0:T(1,128)} %bitcast.5, s32[8]{0:T(128)} %assign_hbm.1), custom_call_target="tpu_custom_call" | custom-call | tf_op jit(solution)/shard_map/pallas_call | solution.py:177
  2.0 3.0 %collective-permute-start.2 = (bf16[776,128]{1,0:T(8,128)(2,1)S(1)}, bf16[776,128]{1,0:T(8,128)(2,1)S(1)}, u32[]{:S(2)}, u32[]{:S(2)}) collective-permute-start(bf16[776,128]{1,0:T(8,128)(2,1)S(1)} %shard_map.55.refs_0_.refs_5_), channel_id=1, source_target_pairs={{2,0},{3,1},{0,2},{1,3},{6,4},{7,5},{4,6},{5,7},{10,8},{11,9},{8,1... | collective-permute-start | bytes 595976 | tf_op jit(solution)/shard_map/ppermute | solution.py:253
  5.1 0.0 collective-permute-start.3
  5.1 4.9 %collective-permute-done.2.refs_2_ = bf16[776,128]{1,0:T(8,128)(2,1)S(1)} collective-permute-done((bf16[776,128]{1,0:T(8,128)(2,1)S(1)}, bf16[776,128]{1,0:T(8,128)(2,1)S(1)}, u32[]{:S(2)}, u32[]{:S(2)}) %collective-permute-start.2) | collective-permute-done | bytes 198688 | tf_op jit(solution)/shard_map/ppermute | solution.py:253
  10.0 0.0 collective-permute-start.4
  10.0 3.8 %collective-permute-start = (bf16[776,128]{1,0:T(8,128)(2,1)S(1)}, bf16[776,128]{1,0:T(8,128)(2,1)S(1)}, u32[]{:S(2)}, u32[]{:S(2)}) collective-permute-start(bf16[776,128]{1,0:T(8,128)(2,1)S(1)} %shard_map.55.refs_0_.refs_5_), channel_id=1, source_target_pairs={{8,0},{9,1},{10,2},{11,3},{12,4},{13,5},{14,6},{15,7},{4,8},{5,9},... | collective-permute-start | bytes 595976 | tf_op jit(solution)/shard_map/ppermute | solution.py:253
  13.9 0.0 collective-permute-start.1
  13.9 0.0 collective-permute-done.3.refs_1_.refs_3_
  13.9 0.0 collective-permute-done.4.refs_3_.refs_4_
  13.9 0.4 %shard_map.56.refs_6_ = f32[1,128]{1,0:T(1,128)S(1)} custom-call(bf16[776,128]{1,0:T(8,128)(2,1)S(1)} %shard_map.55.refs_0_.refs_5_, bf16[776,128]{1,0:T(8,128)(2,1)S(1)} %collective-permute-done.3.refs_1_.refs_3_, bf16[776,128]{1,0:T(8,128)(2,1)S(1)} %collective-permute-done.2.refs_2_, bf16[776,128]{1,0:T(8,128)(2,1)S(1)} %collective-permute-done.4.refs_3_.refs_4_), custom_call_target="tpu_custom_call" | custom-call | tf_op jit(solution)/shard_map/pallas_call | solution.py:242
  14.3 8.6 %collective-permute-done.refs_0_.refs_4_ = bf16[776,128]{1,0:T(8,128)(2,1)S(1)} collective-permute-done((bf16[776,128]{1,0:T(8,128)(2,1)S(1)}, bf16[776,128]{1,0:T(8,128)(2,1)S(1)}, u32[]{:S(2)}, u32[]{:S(2)}) %collective-permute-start) | collective-permute-done | bytes 198688 | tf_op jit(solution)/shard_map/ppermute | solution.py:253
  22.8 1.2 %collective-permute-done.1.refs_1_ = bf16[776,128]{1,0:T(8,128)(2,1)S(1)} collective-permute-done((bf16[776,128]{1,0:T(8,128)(2,1)S(1)}, bf16[776,128]{1,0:T(8,128)(2,1)S(1)}, u32[]{:S(2)}, u32[]{:S(2)}) %collective-permute-start.1) | collective-permute-done | bytes 198688 | tf_op jit(solution)/shard_map/ppermute | solution.py:253
  24.0 0.6 %shard_map.57 = (f32[1,128]{1,0:T(1,128)S(1)}, f32[1,128]{1,0:T(1,128)S(1)}, f32[1,128]{1,0:T(1,128)S(1)}, f32[1,128]{1,0:T(1,128)S(1)}) custom-call(bf16[776,128]{1,0:T(8,128)(2,1)S(1)} %collective-permute-done.refs_0_.refs_4_, bf16[776,128]{1,0:T(8,128)(2,1)S(1)} %collective-permute-done.1.refs_1_, bf16[776,128]{1,0:T(8,128)(2,1)S(1)} %collective-permute-done.2.refs_2_, ...), custom_call_target="tpu_custom_call" | custom-call | tf_op jit(solution)/shard_map/pallas_call | solution.py:242
  24.6 0.1 collective-permute-start.8
  24.7 1.6 %collective-permute-start.7 = (f32[1,128]{1,0:T(1,128)S(1)}, f32[1,128]{1,0:T(1,128)S(1)}, u32[]{:S(2)}, u32[]{:S(2)}) collective-permute-start(f32[1,128]{1,0:T(1,128)S(1)} %get-tuple-element.11), channel_id=1, source_target_pairs={{0,3},{1,2},{2,1},{3,0},{4,7},{5,6},{6,5},{7,4},{8,11},{9,10},{10,... | collective-permute-start | bytes 1544 | tf_op jit(solution)/shard_map/ppermute | solution.py:253
  26.4 0.5 %collective-permute-start.6 = (f32[1,128]{1,0:T(1,128)S(1)}, f32[1,128]{1,0:T(1,128)S(1)}, u32[]{:S(2)}, u32[]{:S(2)}) collective-permute-start(f32[1,128]{1,0:T(1,128)S(1)} %get-tuple-element.10), channel_id=1, source_target_pairs={{0,2},{1,3},{2,0},{3,1},{4,6},{5,7},{6,4},{7,5},{8,10},{9,11},{10,... | collective-permute-start | bytes 1544 | tf_op jit(solution)/shard_map/ppermute | solution.py:253
  26.8 0.4 %shard_map.58 = f32[1,128]{1,0:T(1,128)S(1)} custom-call(bf16[776,128]{1,0:T(8,128)(2,1)S(1)} %shard_map.55.refs_0_.refs_5_, bf16[776,128]{1,0:T(8,128)(2,1)S(1)} %collective-permute-done.3.refs_1_.refs_3_, bf16[776,128]{1,0:T(8,128)(2,1)S(1)} %collective-permute-done.2.refs_2_, bf16[776,128]{1,0:T(8,128)(2,1)S(1)} %collective-permute-done.4.refs_3_.refs_4_, ...), custom_call_target="tpu_custom_call" | custom-call | tf_op jit(solution)/shard_map/pallas_call | solution.py:242
  27.2 0.5 %collective-permute-start.5 = (f32[1,128]{1,0:T(1,128)S(1)}, f32[1,128]{1,0:T(1,128)S(1)}, u32[]{:S(2)}, u32[]{:S(2)}) collective-permute-start(f32[1,128]{1,0:T(1,128)S(1)} %shard_map.58), channel_id=1, source_target_pairs={{0,8},{1,9},{2,10},{3,11},{4,12},{5,13},{6,14},{7,15},{8,4},{9,5},... | collective-permute-start | bytes 1544 | tf_op jit(solution)/shard_map/ppermute | solution.py:253
  27.7 0.0 collective-permute-done.8
  27.7 0.1 collective-permute-done.7
  27.8 2.2 %collective-permute-done.6 = f32[1,128]{1,0:T(1,128)S(1)} collective-permute-done((f32[1,128]{1,0:T(1,128)S(1)}, f32[1,128]{1,0:T(1,128)S(1)}, u32[]{:S(2)}, u32[]{:S(2)}) %collective-permute-start.6) | collective-permute-done | bytes 544 | tf_op jit(solution)/shard_map/ppermute | solution.py:253
  29.9 2.7 %collective-permute-done.5 = f32[1,128]{1,0:T(1,128)S(1)} collective-permute-done((f32[1,128]{1,0:T(1,128)S(1)}, f32[1,128]{1,0:T(1,128)S(1)}, u32[]{:S(2)}, u32[]{:S(2)}) %collective-permute-start.5) | collective-permute-done | bytes 544 | tf_op jit(solution)/shard_map/ppermute | solution.py:253
  32.6 0.5 %maximum_bitcast_fusion = f32[128]{0:T(128)} fusion(f32[1,128]{1,0:T(1,128)S(1)} %collective-permute-done.8, f32[1,128]{1,0:T(1,128)S(1)} %collective-permute-done.7, f32[1,128]{1,0:T(1,128)S(1)} %collective-permute-done.6, f32[1,128]{1,0:T(1,128)S(1)} %get-tuple-element.9, f32[1,128]{1,0:T(1,128)S(1)} %collective-permute-done.5), kind=kLoop, calls=%fused_computation | loop fusion | flops 512 | bytes 3072 | tf_op jit(solution)/shard_map/reshape | solution.py:273
Async XLA Ops:
  2.0 8.0 %collective-permute-start.2 = (bf16[776,128]{1,0:T(8,128)(2,1)S(1)}, bf16[776,128]{1,0:T(8,128)(2,1)S(1)}, u32[]{:S(2)}, u32[]{:S(2)}) collective-permute-start(bf16[776,128]{1,0:T(8,128)(2,1)S(1)} %shard_map.55.refs_0_.refs_5_), channel_id=1, source_target_pairs={{2,0},{3,1},{0,2},{1,3},{6,4},{7,5},{4,6},{5,7},{10,8},{11,9},{8,1... | collective-permute-start | bytes 595976 | tf_op jit(solution)/shard_map/ppermute | solution.py:253
  5.1 8.8 %collective-permute-start.3 = (bf16[776,128]{1,0:T(8,128)(2,1)S(1)}, bf16[776,128]{1,0:T(8,128)(2,1)S(1)}, u32[]{:S(2)}, u32[]{:S(2)}) collective-permute-start(bf16[776,128]{1,0:T(8,128)(2,1)S(1)} %shard_map.55.refs_0_.refs_5_), channel_id=1, source_target_pairs={{1,0},{0,1},{3,2},{2,3},{5,4},{4,5},{7,6},{6,7},{9,8},{8,9},{11,10... | collective-permute-start | bytes 595976 | tf_op jit(solution)/shard_map/ppermute | solution.py:253
  10.0 3.9 %collective-permute-start.4 = (bf16[776,128]{1,0:T(8,128)(2,1)S(1)}, bf16[776,128]{1,0:T(8,128)(2,1)S(1)}, u32[]{:S(2)}, u32[]{:S(2)}) collective-permute-start(bf16[776,128]{1,0:T(8,128)(2,1)S(1)} %collective-permute-done.2.refs_2_), channel_id=1, source_target_pairs={{1,0},{0,1},{3,2},{2,3},{5,4},{4,5},{7,6},{6,7},{9,8},{8,9},{11,10... | collective-permute-start | bytes 595976 | tf_op jit(solution)/shard_map/ppermute | solution.py:253
  10.0 12.8 %collective-permute-start = (bf16[776,128]{1,0:T(8,128)(2,1)S(1)}, bf16[776,128]{1,0:T(8,128)(2,1)S(1)}, u32[]{:S(2)}, u32[]{:S(2)}) collective-permute-start(bf16[776,128]{1,0:T(8,128)(2,1)S(1)} %shard_map.55.refs_0_.refs_5_), channel_id=1, source_target_pairs={{8,0},{9,1},{10,2},{11,3},{12,4},{13,5},{14,6},{15,7},{4,8},{5,9},... | collective-permute-start | bytes 595976 | tf_op jit(solution)/shard_map/ppermute | solution.py:253
  13.9 10.2 %collective-permute-start.1 = (bf16[776,128]{1,0:T(8,128)(2,1)S(1)}, bf16[776,128]{1,0:T(8,128)(2,1)S(1)}, u32[]{:S(2)}, u32[]{:S(2)}) collective-permute-start(bf16[776,128]{1,0:T(8,128)(2,1)S(1)} %shard_map.55.refs_0_.refs_5_), channel_id=1, source_target_pairs={{4,0},{5,1},{6,2},{7,3},{0,4},{1,5},{2,6},{3,7},{12,8},{13,9},{14,... | collective-permute-start | bytes 595976 | tf_op jit(solution)/shard_map/ppermute | solution.py:253
  24.6 3.1 %collective-permute-start.8 = (f32[1,128]{1,0:T(1,128)S(1)}, f32[1,128]{1,0:T(1,128)S(1)}, u32[]{:S(2)}, u32[]{:S(2)}) collective-permute-start(f32[1,128]{1,0:T(1,128)S(1)} %get-tuple-element.12), channel_id=1, source_target_pairs={{0,1},{1,0},{2,3},{3,2},{4,5},{5,4},{6,7},{7,6},{8,9},{9,8},{10,11... | collective-permute-start | bytes 1544 | tf_op jit(solution)/shard_map/ppermute | solution.py:253
  24.7 3.1 %collective-permute-start.7 = (f32[1,128]{1,0:T(1,128)S(1)}, f32[1,128]{1,0:T(1,128)S(1)}, u32[]{:S(2)}, u32[]{:S(2)}) collective-permute-start(f32[1,128]{1,0:T(1,128)S(1)} %get-tuple-element.11), channel_id=1, source_target_pairs={{0,3},{1,2},{2,1},{3,0},{4,7},{5,6},{6,5},{7,4},{8,11},{9,10},{10,... | collective-permute-start | bytes 1544 | tf_op jit(solution)/shard_map/ppermute | solution.py:253
  26.4 3.6 %collective-permute-start.6 = (f32[1,128]{1,0:T(1,128)S(1)}, f32[1,128]{1,0:T(1,128)S(1)}, u32[]{:S(2)}, u32[]{:S(2)}) collective-permute-start(f32[1,128]{1,0:T(1,128)S(1)} %get-tuple-element.10), channel_id=1, source_target_pairs={{0,2},{1,3},{2,0},{3,1},{4,6},{5,7},{6,4},{7,5},{8,10},{9,11},{10,... | collective-permute-start | bytes 1544 | tf_op jit(solution)/shard_map/ppermute | solution.py:253
  27.2 5.4 %collective-permute-start.5 = (f32[1,128]{1,0:T(1,128)S(1)}, f32[1,128]{1,0:T(1,128)S(1)}, u32[]{:S(2)}, u32[]{:S(2)}) collective-permute-start(f32[1,128]{1,0:T(1,128)S(1)} %shard_map.58), channel_id=1, source_target_pairs={{0,8},{1,9},{2,10},{3,11},{4,12},{5,13},{6,14},{7,15},{8,4},{9,5},... | collective-permute-start | bytes 1544 | tf_op jit(solution)/shard_map/ppermute | solution.py:253

commit v4 on v3

--- a/solution.py
+++ b/solution.py
@@ -256,14 +256,14 @@
 def covered(plan, n_dp, images, cls_feats, proj, cluster_id, row_index, assign):
     sources, pairs = plan
     perms = [[(h[slot], d) for d, h in enumerate(sources)] for slot in range(FAR + 1)]
-    early = [(q, c) for q, c in pairs if max(q, c) < NEAR]
-    rest = [(q, c) for q, c in pairs if q < NEAR <= c]
+    early = [(q, c) for q, c in pairs if max(q, c) < PEER]
+    rest = [(q, c) for q, c in pairs if q < FAR and max(q, c) >= PEER]
     own = embed(cls_feats, proj, cluster_id, row_index, assign, assign.shape[0] // n_dp)
     held = {slot: permute(own, perms[slot]) for slot in (FAR, NEAR, SIDE, CORE)}
     held[PEER] = permute(held[SIDE], perms[CORE])
     held[OWN] = own
     plane = {slot: held[slot] for slot in (OWN, CORE, SIDE, PEER)}
-    best = scores(plane, early, images)
+    best = scores({i: plane[i] for i in (OWN, CORE, SIDE)}, early, images)
     best |= scores(plane | {FAR: held[FAR]}, [(q, c) for q, c in pairs if q == FAR], images)
     best |= scores(held, rest, images, {OWN: best[OWN]})
     total = best[OWN]

time: 33.3 us -> 28.2 us (0.85)
  waiting for transfers between devices: 19.7 us -> 14.9 us
    ppermute x9, waiting for transfers between devices: 19.7 us -> 14.9 us  [permute(): return lax.ppermute(value, GROUP, pairs)]
  transfers between devices with their start and end apart: 9 -> 9, of which waited for: 6 -> 6; matrix products, arithmetic and copies ran while one was open for 0% -> 0% of each run, Pallas kernels for 2% -> 3%
where the time goes in v4:
time: 28.2 us; the launch traced here: 28.1 us
  waiting for transfers between devices  14.9 us (53%)
  starting transfers between devices  9.26 us (33%)
  Pallas kernels  3.41 us (12%)
  other arithmetic  0.52 us (2%)
    ppermute x9, waiting for transfers between devices, permute(): return lax.ppermute(value, GROUP, pairs)  14.9 us
    ppermute x9, starting transfers between devices, permute(): return lax.ppermute(value, GROUP, pairs)  9.26 us
    pallas_call x1, Pallas kernels, embed(): pl.pallas_call(functools.partial(embed_kernel, per_coarse), out_shape=jax...  2.03 us
    pallas_call x3, Pallas kernels, scores(): pl.pallas_call(functools.partial(score_kernel, images, len(names), wanted...  1.38 us
  transfers between devices with their start and end apart: 9, of which 6 were waited for; matrix products, arithmetic and copies ran while one was open for 0% of the time, Pallas kernels for 3%

profile of v4, /device:TPU:0, one launch (start us, length us, event | category | flops | bytes accessed | tf_op | source)
XLA Modules:
  0.0 28.1 jit_solution(17680468321163980034)
XLA Ops:
  0.0 2.0 %shard_map.55.refs_0_.refs_5_ = bf16[776,128]{1,0:T(8,128)(2,1)S(1)} custom-call(bf16[128,1024]{1,0:T(8,128)(2,1)} %cls_hbm.1, bf16[1024,768]{1,0:T(8,128)(2,1)} %proj_hbm.1, s32[1,128]{1,0:T(1,128)} %bitcast.4, s32[1,128]{1,0:T(1,128)} %bitcast.5, s32[8]{0:T(128)} %assign_hbm.1), custom_call_target="tpu_custom_call" | custom-call | tf_op jit(solution)/shard_map/pallas_call | solution.py:177
  2.0 3.0 %collective-permute-start.2 = (bf16[776,128]{1,0:T(8,128)(2,1)S(1)}, bf16[776,128]{1,0:T(8,128)(2,1)S(1)}, u32[]{:S(2)}, u32[]{:S(2)}) collective-permute-start(bf16[776,128]{1,0:T(8,128)(2,1)S(1)} %shard_map.55.refs_0_.refs_5_), channel_id=1, source_target_pairs={{2,0},{3,1},{0,2},{1,3},{6,4},{7,5},{4,6},{5,7},{10,8},{11,9},{8,1... | collective-permute-start | bytes 595976 | tf_op jit(solution)/shard_map/ppermute | solution.py:253
  5.1 0.0 collective-permute-start.3
  5.1 3.6 %collective-permute-start = (bf16[776,128]{1,0:T(8,128)(2,1)S(1)}, bf16[776,128]{1,0:T(8,128)(2,1)S(1)}, u32[]{:S(2)}, u32[]{:S(2)}) collective-permute-start(bf16[776,128]{1,0:T(8,128)(2,1)S(1)} %shard_map.55.refs_0_.refs_5_), channel_id=1, source_target_pairs={{8,0},{9,1},{10,2},{11,3},{12,4},{13,5},{14,6},{15,7},{4,8},{5,9},... | collective-permute-start | bytes 595976 | tf_op jit(solution)/shard_map/ppermute | solution.py:253
  8.7 0.0 collective-permute-start.1
  8.7 1.3 %collective-permute-done.2.refs_2_ = bf16[776,128]{1,0:T(8,128)(2,1)S(1)} collective-permute-done((bf16[776,128]{1,0:T(8,128)(2,1)S(1)}, bf16[776,128]{1,0:T(8,128)(2,1)S(1)}, u32[]{:S(2)}, u32[]{:S(2)}) %collective-permute-start.2) | collective-permute-done | bytes 198688 | tf_op jit(solution)/shard_map/ppermute | solution.py:253
  10.0 0.0 collective-permute-start.4
  10.0 0.0 collective-permute-done.3.refs_1_.refs_3_
  10.0 0.3 %shard_map.56.refs_6_ = f32[1,128]{1,0:T(1,128)S(1)} custom-call(bf16[776,128]{1,0:T(8,128)(2,1)S(1)} %shard_map.55.refs_0_.refs_5_, bf16[776,128]{1,0:T(8,128)(2,1)S(1)} %collective-permute-done.3.refs_1_.refs_3_, bf16[776,128]{1,0:T(8,128)(2,1)S(1)} %collective-permute-done.2.refs_2_), custom_call_target="tpu_custom_call" | custom-call | tf_op jit(solution)/shard_map/pallas_call | solution.py:242
  10.4 7.3 %collective-permute-done.refs_0_.refs_4_ = bf16[776,128]{1,0:T(8,128)(2,1)S(1)} collective-permute-done((bf16[776,128]{1,0:T(8,128)(2,1)S(1)}, bf16[776,128]{1,0:T(8,128)(2,1)S(1)}, u32[]{:S(2)}, u32[]{:S(2)}) %collective-permute-start) | collective-permute-done | bytes 198688 | tf_op jit(solution)/shard_map/ppermute | solution.py:253
  17.7 1.2 %collective-permute-done.1.refs_1_ = bf16[776,128]{1,0:T(8,128)(2,1)S(1)} collective-permute-done((bf16[776,128]{1,0:T(8,128)(2,1)S(1)}, bf16[776,128]{1,0:T(8,128)(2,1)S(1)}, u32[]{:S(2)}, u32[]{:S(2)}) %collective-permute-start.1) | collective-permute-done | bytes 198688 | tf_op jit(solution)/shard_map/ppermute | solution.py:253
  18.9 0.0 collective-permute-done.4.refs_4_.refs_3_
  18.9 0.7 %shard_map.57 = (f32[1,128]{1,0:T(1,128)S(1)}, f32[1,128]{1,0:T(1,128)S(1)}, f32[1,128]{1,0:T(1,128)S(1)}, f32[1,128]{1,0:T(1,128)S(1)}) custom-call(bf16[776,128]{1,0:T(8,128)(2,1)S(1)} %collective-permute-done.refs_0_.refs_4_, bf16[776,128]{1,0:T(8,128)(2,1)S(1)} %collective-permute-done.1.refs_1_, bf16[776,128]{1,0:T(8,128)(2,1)S(1)} %collective-permute-done.2.refs_2_, ...), custom_call_target="tpu_custom_call" | custom-call | tf_op jit(solution)/shard_map/pallas_call | solution.py:242
  19.6 0.1 collective-permute-start.8
  19.6 0.6 %collective-permute-start.7 = (f32[1,128]{1,0:T(1,128)S(1)}, f32[1,128]{1,0:T(1,128)S(1)}, u32[]{:S(2)}, u32[]{:S(2)}) collective-permute-start(f32[1,128]{1,0:T(1,128)S(1)} %get-tuple-element.11), channel_id=1, source_target_pairs={{0,3},{1,2},{2,1},{3,0},{4,7},{5,6},{6,5},{7,4},{8,11},{9,10},{10,... | collective-permute-start | bytes 1544 | tf_op jit(solution)/shard_map/ppermute | solution.py:253
  20.2 1.5 %collective-permute-start.6 = (f32[1,128]{1,0:T(1,128)S(1)}, f32[1,128]{1,0:T(1,128)S(1)}, u32[]{:S(2)}, u32[]{:S(2)}) collective-permute-start(f32[1,128]{1,0:T(1,128)S(1)} %get-tuple-element.10), channel_id=1, source_target_pairs={{0,2},{1,3},{2,0},{3,1},{4,6},{5,7},{6,4},{7,5},{8,10},{9,11},{10,... | collective-permute-start | bytes 1544 | tf_op jit(solution)/shard_map/ppermute | solution.py:253
  21.8 0.4 %shard_map.58 = f32[1,128]{1,0:T(1,128)S(1)} custom-call(bf16[776,128]{1,0:T(8,128)(2,1)S(1)} %shard_map.55.refs_0_.refs_5_, bf16[776,128]{1,0:T(8,128)(2,1)S(1)} %collective-permute-done.3.refs_1_.refs_3_, bf16[776,128]{1,0:T(8,128)(2,1)S(1)} %collective-permute-done.2.refs_2_, bf16[776,128]{1,0:T(8,128)(2,1)S(1)} %collective-permute-done.4.refs_4_.refs_3_, ...), custom_call_target="tpu_custom_call" | custom-call | tf_op jit(solution)/shard_map/pallas_call | solution.py:242
  22.2 0.4 %collective-permute-start.5 = (f32[1,128]{1,0:T(1,128)S(1)}, f32[1,128]{1,0:T(1,128)S(1)}, u32[]{:S(2)}, u32[]{:S(2)}) collective-permute-start(f32[1,128]{1,0:T(1,128)S(1)} %shard_map.58), channel_id=1, source_target_pairs={{0,8},{1,9},{2,10},{3,11},{4,12},{5,13},{6,14},{7,15},{8,4},{9,5},... | collective-permute-start | bytes 1544 | tf_op jit(solution)/shard_map/ppermute | solution.py:253
  22.6 0.0 collective-permute-done.8
  22.6 0.1 collective-permute-done.7
  22.7 1.1 %collective-permute-done.6 = f32[1,128]{1,0:T(1,128)S(1)} collective-permute-done((f32[1,128]{1,0:T(1,128)S(1)}, f32[1,128]{1,0:T(1,128)S(1)}, u32[]{:S(2)}, u32[]{:S(2)}) %collective-permute-start.6) | collective-permute-done | bytes 544 | tf_op jit(solution)/shard_map/ppermute | solution.py:253
  23.8 3.8 %collective-permute-done.5 = f32[1,128]{1,0:T(1,128)S(1)} collective-permute-done((f32[1,128]{1,0:T(1,128)S(1)}, f32[1,128]{1,0:T(1,128)S(1)}, u32[]{:S(2)}, u32[]{:S(2)}) %collective-permute-start.5) | collective-permute-done | bytes 544 | tf_op jit(solution)/shard_map/ppermute | solution.py:253
  27.6 0.5 %maximum_bitcast_fusion = f32[128]{0:T(128)} fusion(f32[1,128]{1,0:T(1,128)S(1)} %collective-permute-done.8, f32[1,128]{1,0:T(1,128)S(1)} %collective-permute-done.7, f32[1,128]{1,0:T(1,128)S(1)} %collective-permute-done.6, f32[1,128]{1,0:T(1,128)S(1)} %get-tuple-element.9, f32[1,128]{1,0:T(1,128)S(1)} %collective-permute-done.5), kind=kLoop, calls=%fused_computation | loop fusion | flops 512 | bytes 3072 | tf_op jit(solution)/shard_map/reshape | solution.py:273
Async XLA Ops:
  2.0 8.0 %collective-permute-start.2 = (bf16[776,128]{1,0:T(8,128)(2,1)S(1)}, bf16[776,128]{1,0:T(8,128)(2,1)S(1)}, u32[]{:S(2)}, u32[]{:S(2)}) collective-permute-start(bf16[776,128]{1,0:T(8,128)(2,1)S(1)} %shard_map.55.refs_0_.refs_5_), channel_id=1, source_target_pairs={{2,0},{3,1},{0,2},{1,3},{6,4},{7,5},{4,6},{5,7},{10,8},{11,9},{8,1... | collective-permute-start | bytes 595976 | tf_op jit(solution)/shard_map/ppermute | solution.py:253
  5.1 5.0 %collective-permute-start.3 = (bf16[776,128]{1,0:T(8,128)(2,1)S(1)}, bf16[776,128]{1,0:T(8,128)(2,1)S(1)}, u32[]{:S(2)}, u32[]{:S(2)}) collective-permute-start(bf16[776,128]{1,0:T(8,128)(2,1)S(1)} %shard_map.55.refs_0_.refs_5_), channel_id=1, source_target_pairs={{1,0},{0,1},{3,2},{2,3},{5,4},{4,5},{7,6},{6,7},{9,8},{8,9},{11,10... | collective-permute-start | bytes 595976 | tf_op jit(solution)/shard_map/ppermute | solution.py:253
  5.1 12.6 %collective-permute-start = (bf16[776,128]{1,0:T(8,128)(2,1)S(1)}, bf16[776,128]{1,0:T(8,128)(2,1)S(1)}, u32[]{:S(2)}, u32[]{:S(2)}) collective-permute-start(bf16[776,128]{1,0:T(8,128)(2,1)S(1)} %shard_map.55.refs_0_.refs_5_), channel_id=1, source_target_pairs={{8,0},{9,1},{10,2},{11,3},{12,4},{13,5},{14,6},{15,7},{4,8},{5,9},... | collective-permute-start | bytes 595976 | tf_op jit(solution)/shard_map/ppermute | solution.py:253
  8.7 10.2 %collective-permute-start.1 = (bf16[776,128]{1,0:T(8,128)(2,1)S(1)}, bf16[776,128]{1,0:T(8,128)(2,1)S(1)}, u32[]{:S(2)}, u32[]{:S(2)}) collective-permute-start(bf16[776,128]{1,0:T(8,128)(2,1)S(1)} %shard_map.55.refs_0_.refs_5_), channel_id=1, source_target_pairs={{4,0},{5,1},{6,2},{7,3},{0,4},{1,5},{2,6},{3,7},{12,8},{13,9},{14,... | collective-permute-start | bytes 595976 | tf_op jit(solution)/shard_map/ppermute | solution.py:253
  10.0 8.9 %collective-permute-start.4 = (bf16[776,128]{1,0:T(8,128)(2,1)S(1)}, bf16[776,128]{1,0:T(8,128)(2,1)S(1)}, u32[]{:S(2)}, u32[]{:S(2)}) collective-permute-start(bf16[776,128]{1,0:T(8,128)(2,1)S(1)} %collective-permute-done.2.refs_2_), channel_id=1, source_target_pairs={{1,0},{0,1},{3,2},{2,3},{5,4},{4,5},{7,6},{6,7},{9,8},{8,9},{11,10... | collective-permute-start | bytes 595976 | tf_op jit(solution)/shard_map/ppermute | solution.py:253
  19.6 3.0 %collective-permute-start.8 = (f32[1,128]{1,0:T(1,128)S(1)}, f32[1,128]{1,0:T(1,128)S(1)}, u32[]{:S(2)}, u32[]{:S(2)}) collective-permute-start(f32[1,128]{1,0:T(1,128)S(1)} %get-tuple-element.12), channel_id=1, source_target_pairs={{0,1},{1,0},{2,3},{3,2},{4,5},{5,4},{6,7},{7,6},{8,9},{9,8},{10,11... | collective-permute-start | bytes 1544 | tf_op jit(solution)/shard_map/ppermute | solution.py:253
  19.6 3.1 %collective-permute-start.7 = (f32[1,128]{1,0:T(1,128)S(1)}, f32[1,128]{1,0:T(1,128)S(1)}, u32[]{:S(2)}, u32[]{:S(2)}) collective-permute-start(f32[1,128]{1,0:T(1,128)S(1)} %get-tuple-element.11), channel_id=1, source_target_pairs={{0,3},{1,2},{2,1},{3,0},{4,7},{5,6},{6,5},{7,4},{8,11},{9,10},{10,... | collective-permute-start | bytes 1544 | tf_op jit(solution)/shard_map/ppermute | solution.py:253
  20.2 3.6 %collective-permute-start.6 = (f32[1,128]{1,0:T(1,128)S(1)}, f32[1,128]{1,0:T(1,128)S(1)}, u32[]{:S(2)}, u32[]{:S(2)}) collective-permute-start(f32[1,128]{1,0:T(1,128)S(1)} %get-tuple-element.10), channel_id=1, source_target_pairs={{0,2},{1,3},{2,0},{3,1},{4,6},{5,7},{6,4},{7,5},{8,10},{9,11},{10,... | collective-permute-start | bytes 1544 | tf_op jit(solution)/shard_map/ppermute | solution.py:253
  22.2 5.4 %collective-permute-start.5 = (f32[1,128]{1,0:T(1,128)S(1)}, f32[1,128]{1,0:T(1,128)S(1)}, u32[]{:S(2)}, u32[]{:S(2)}) collective-permute-start(f32[1,128]{1,0:T(1,128)S(1)} %shard_map.58), channel_id=1, source_target_pairs={{0,8},{1,9},{2,10},{3,11},{4,12},{5,13},{6,14},{7,15},{8,4},{9,5},... | collective-permute-start | bytes 1544 | tf_op jit(solution)/shard_map/ppermute | solution.py:253

commit v5 on v4

--- a/solution.py
+++ b/solution.py
@@ -172,7 +172,7 @@
 def embed(cls_feats, proj, cluster_id, row_index, assign, per_coarse):
     rows, depth = cls_feats.shape
     width = proj.shape[1]
-    chunks = 4
+    chunks = 2
     args = (cls_feats, proj, cluster_id.reshape(1, rows), row_index.reshape(1, rows), assign)
     return pl.pallas_call(
         functools.partial(embed_kernel, per_coarse),
@@ -258,6 +258,7 @@
     perms = [[(h[slot], d) for d, h in enumerate(sources)] for slot in range(FAR + 1)]
     early = [(q, c) for q, c in pairs if max(q, c) < PEER]
     rest = [(q, c) for q, c in pairs if q < FAR and max(q, c) >= PEER]
+    sooner, later = (PEER, SIDE), (OWN, CORE)
     own = embed(cls_feats, proj, cluster_id, row_index, assign, assign.shape[0] // n_dp)
     held = {slot: permute(own, perms[slot]) for slot in (FAR, NEAR, SIDE, CORE)}
     held[PEER] = permute(held[SIDE], perms[CORE])
@@ -265,7 +266,11 @@
     plane = {slot: held[slot] for slot in (OWN, CORE, SIDE, PEER)}
     best = scores({i: plane[i] for i in (OWN, CORE, SIDE)}, early, images)
     best |= scores(plane | {FAR: held[FAR]}, [(q, c) for q, c in pairs if q == FAR], images)
-    best |= scores(held, rest, images, {OWN: best[OWN]})
+    for group in (sooner, later):
+        part = [(q, c) for q, c in rest if q in group]
+        used = {i: held[i] for i in held if any(i in pair for pair in part)}
+        before = {OWN: best[OWN]} if OWN in group else {}
+        best |= scores(used, part, images, before)
     total = best[OWN]
     for slot in (FAR, SIDE, PEER, CORE):
         back = [(b, a) for a, b in perms[slot]]

time: 28.2 us -> 28.2 us (level)
  waiting for transfers between devices: 14.9 us -> 13.2 us
  starting transfers between devices: 9.26 us -> 10.8 us
    ppermute x9, waiting for transfers between devices: 14.9 us -> 13.2 us  [permute(): return lax.ppermute(value, GROUP, pairs)]
    ppermute x9, starting transfers between devices: 9.26 us -> 10.8 us  [permute(): return lax.ppermute(value, GROUP, pairs)]
    pallas_call x3 -> x4, Pallas kernels: 1.38 us -> 1.53 us  [scores(): pl.pallas_call(functools.partial(score_kernel, images, len(names), wanted...]
  transfers between devices with their start and end apart: 9 -> 9, of which waited for: 6 -> 4; matrix products, arithmetic and copies ran while one was open for 0% -> 0% of each run, Pallas kernels for 3% -> 4%
where the time goes in v5:
time: 28.2 us; the launch traced here: 28 us
  waiting for transfers between devices  13.2 us (47%)
  starting transfers between devices  10.8 us (38%)
  Pallas kernels  3.5 us (12%)
  other arithmetic  0.52 us (2%)
    ppermute x9, waiting for transfers between devices, permute(): return lax.ppermute(value, GROUP, pairs)  13.2 us
    ppermute x9, starting transfers between devices, permute(): return lax.ppermute(value, GROUP, pairs)  10.8 us
    pallas_call x1, Pallas kernels, embed(): pl.pallas_call(functools.partial(embed_kernel, per_coarse), out_shape=jax...  1.98 us
    pallas_call x4, Pallas kernels, scores(): pl.pallas_call(functools.partial(score_kernel, images, len(names), wanted...  1.53 us
  transfers between devices with their start and end apart: 9, of which 4 were waited for; matrix products, arithmetic and copies ran while one was open for 0% of the time, Pallas kernels for 4%

profile of v5, /device:TPU:0, one launch (start us, length us, event | category | flops | bytes accessed | tf_op | source)
XLA Modules:
  0.0 28.0 jit_solution(4132848509390985853)
XLA Ops:
  0.0 2.0 %shard_map.55.refs_0_.refs_4_ = bf16[776,128]{1,0:T(8,128)(2,1)S(1)} custom-call(bf16[128,1024]{1,0:T(8,128)(2,1)} %cls_hbm.1, bf16[1024,768]{1,0:T(8,128)(2,1)} %proj_hbm.1, s32[1,128]{1,0:T(1,128)} %bitcast.4, s32[1,128]{1,0:T(1,128)} %bitcast.5, s32[8]{0:T(128)} %assign_hbm.1), custom_call_target="tpu_custom_call" | custom-call | tf_op jit(solution)/shard_map/pallas_call | solution.py:177
  2.0 3.0 %collective-permute-start.3 = (bf16[776,128]{1,0:T(8,128)(2,1)S(1)}, bf16[776,128]{1,0:T(8,128)(2,1)S(1)}, u32[]{:S(2)}, u32[]{:S(2)}) collective-permute-start(bf16[776,128]{1,0:T(8,128)(2,1)S(1)} %shard_map.55.refs_0_.refs_4_), channel_id=1, source_target_pairs={{2,0},{3,1},{0,2},{1,3},{6,4},{7,5},{4,6},{5,7},{10,8},{11,9},{8,1... | collective-permute-start | bytes 595976 | tf_op jit(solution)/shard_map/ppermute | solution.py:253
  5.0 0.0 collective-permute-start.2
  5.0 1.6 %collective-permute-start.1 = (bf16[776,128]{1,0:T(8,128)(2,1)S(1)}, bf16[776,128]{1,0:T(8,128)(2,1)S(1)}, u32[]{:S(2)}, u32[]{:S(2)}) collective-permute-start(bf16[776,128]{1,0:T(8,128)(2,1)S(1)} %shard_map.55.refs_0_.refs_4_), channel_id=1, source_target_pairs={{4,0},{5,1},{6,2},{7,3},{0,4},{1,5},{2,6},{3,7},{12,8},{13,9},{14,... | collective-permute-start | bytes 595976 | tf_op jit(solution)/shard_map/ppermute | solution.py:253
  6.6 2.5 %collective-permute-start = (bf16[776,128]{1,0:T(8,128)(2,1)S(1)}, bf16[776,128]{1,0:T(8,128)(2,1)S(1)}, u32[]{:S(2)}, u32[]{:S(2)}) collective-permute-start(bf16[776,128]{1,0:T(8,128)(2,1)S(1)} %shard_map.55.refs_0_.refs_4_), channel_id=1, source_target_pairs={{8,0},{9,1},{10,2},{11,3},{12,4},{13,5},{14,6},{15,7},{4,8},{5,9},... | collective-permute-start | bytes 595976 | tf_op jit(solution)/shard_map/ppermute | solution.py:253
  9.1 0.9 %collective-permute-done.3.refs_2_ = bf16[776,128]{1,0:T(8,128)(2,1)S(1)} collective-permute-done((bf16[776,128]{1,0:T(8,128)(2,1)S(1)}, bf16[776,128]{1,0:T(8,128)(2,1)S(1)}, u32[]{:S(2)}, u32[]{:S(2)}) %collective-permute-start.3) | collective-permute-done | bytes 198688 | tf_op jit(solution)/shard_map/ppermute | solution.py:253
  10.0 0.0 collective-permute-start.4
  10.0 0.0 collective-permute-done.2.refs_1_.refs_2_
  10.0 0.3 %shard_map.56.refs_5_ = f32[1,128]{1,0:T(1,128)S(1)} custom-call(bf16[776,128]{1,0:T(8,128)(2,1)S(1)} %shard_map.55.refs_0_.refs_4_, bf16[776,128]{1,0:T(8,128)(2,1)S(1)} %collective-permute-done.2.refs_1_.refs_2_, bf16[776,128]{1,0:T(8,128)(2,1)S(1)} %collective-permute-done.3.refs_2_), custom_call_target="tpu_custom_call" | custom-call | tf_op jit(solution)/shard_map/pallas_call | solution.py:242
  10.3 6.2 %collective-permute-done.1.refs_1_ = bf16[776,128]{1,0:T(8,128)(2,1)S(1)} collective-permute-done((bf16[776,128]{1,0:T(8,128)(2,1)S(1)}, bf16[776,128]{1,0:T(8,128)(2,1)S(1)}, u32[]{:S(2)}, u32[]{:S(2)}) %collective-permute-start.1) | collective-permute-done | bytes 198688 | tf_op jit(solution)/shard_map/ppermute | solution.py:253
  16.5 2.4 %collective-permute-done.refs_0_.refs_4_ = bf16[776,128]{1,0:T(8,128)(2,1)S(1)} collective-permute-done((bf16[776,128]{1,0:T(8,128)(2,1)S(1)}, bf16[776,128]{1,0:T(8,128)(2,1)S(1)}, u32[]{:S(2)}, u32[]{:S(2)}) %collective-permute-start) | collective-permute-done | bytes 198688 | tf_op jit(solution)/shard_map/ppermute | solution.py:253
  18.9 0.0 collective-permute-done.4.refs_3_
  18.9 0.4 %shard_map.57 = (f32[1,128]{1,0:T(1,128)S(1)}, f32[1,128]{1,0:T(1,128)S(1)}) custom-call(bf16[776,128]{1,0:T(8,128)(2,1)S(1)} %collective-permute-done.refs_0_.refs_4_, bf16[776,128]{1,0:T(8,128)(2,1)S(1)} %collective-permute-done.1.refs_1_, bf16[776,128]{1,0:T(8,128)(2,1)S(1)} %collective-permute-done.2.refs_1_.refs_2_, ...), custom_call_target="tpu_custom_call" | custom-call | tf_op jit(solution)/shard_map/pallas_call | solution.py:242
  19.3 0.1 collective-permute-start.8
  19.4 0.4 %shard_map.59 = (f32[1,128]{1,0:T(1,128)S(1)}, f32[1,128]{1,0:T(1,128)S(1)}) custom-call(bf16[776,128]{1,0:T(8,128)(2,1)S(1)} %collective-permute-done.refs_0_.refs_4_, bf16[776,128]{1,0:T(8,128)(2,1)S(1)} %collective-permute-done.1.refs_1_, bf16[776,128]{1,0:T(8,128)(2,1)S(1)} %collective-permute-done.3.refs_2_, ...), custom_call_target="tpu_custom_call" | custom-call | tf_op jit(solution)/shard_map/pallas_call | solution.py:242
  19.8 0.6 %collective-permute-start.6 = (f32[1,128]{1,0:T(1,128)S(1)}, f32[1,128]{1,0:T(1,128)S(1)}, u32[]{:S(2)}, u32[]{:S(2)}) collective-permute-start(f32[1,128]{1,0:T(1,128)S(1)} %get-tuple-element.10), channel_id=1, source_target_pairs={{0,2},{1,3},{2,0},{3,1},{4,6},{5,7},{6,4},{7,5},{8,10},{9,11},{10,... | collective-permute-start | bytes 1544 | tf_op jit(solution)/shard_map/ppermute | solution.py:253
  20.4 1.3 %collective-permute-start.7 = (f32[1,128]{1,0:T(1,128)S(1)}, f32[1,128]{1,0:T(1,128)S(1)}, u32[]{:S(2)}, u32[]{:S(2)}) collective-permute-start(f32[1,128]{1,0:T(1,128)S(1)} %get-tuple-element.11), channel_id=1, source_target_pairs={{0,3},{1,2},{2,1},{3,0},{4,7},{5,6},{6,5},{7,4},{8,11},{9,10},{10,... | collective-permute-start | bytes 1544 | tf_op jit(solution)/shard_map/ppermute | solution.py:253
  21.7 0.4 %shard_map.58 = f32[1,128]{1,0:T(1,128)S(1)} custom-call(bf16[776,128]{1,0:T(8,128)(2,1)S(1)} %shard_map.55.refs_0_.refs_4_, bf16[776,128]{1,0:T(8,128)(2,1)S(1)} %collective-permute-done.2.refs_1_.refs_2_, bf16[776,128]{1,0:T(8,128)(2,1)S(1)} %collective-permute-done.3.refs_2_, bf16[776,128]{1,0:T(8,128)(2,1)S(1)} %collective-permute-done.4.refs_3_, ...), custom_call_target="tpu_custom_call" | custom-call | tf_op jit(solution)/shard_map/pallas_call | solution.py:242
  22.1 1.7 %collective-permute-start.5 = (f32[1,128]{1,0:T(1,128)S(1)}, f32[1,128]{1,0:T(1,128)S(1)}, u32[]{:S(2)}, u32[]{:S(2)}) collective-permute-start(f32[1,128]{1,0:T(1,128)S(1)} %shard_map.58), channel_id=1, source_target_pairs={{0,8},{1,9},{2,10},{3,11},{4,12},{5,13},{6,14},{7,15},{8,4},{9,5},... | collective-permute-start | bytes 1544 | tf_op jit(solution)/shard_map/ppermute | solution.py:253
  23.8 0.0 collective-permute-done.8
  23.8 0.0 collective-permute-done.6
  23.8 0.0 collective-permute-done.7
  23.8 3.7 %collective-permute-done.5 = f32[1,128]{1,0:T(1,128)S(1)} collective-permute-done((f32[1,128]{1,0:T(1,128)S(1)}, f32[1,128]{1,0:T(1,128)S(1)}, u32[]{:S(2)}, u32[]{:S(2)}) %collective-permute-start.5) | collective-permute-done | bytes 544 | tf_op jit(solution)/shard_map/ppermute | solution.py:253
  27.5 0.5 %maximum_bitcast_fusion = f32[128]{0:T(128)} fusion(f32[1,128]{1,0:T(1,128)S(1)} %collective-permute-done.8, f32[1,128]{1,0:T(1,128)S(1)} %collective-permute-done.7, f32[1,128]{1,0:T(1,128)S(1)} %collective-permute-done.6, f32[1,128]{1,0:T(1,128)S(1)} %get-tuple-element.9, f32[1,128]{1,0:T(1,128)S(1)} %collective-permute-done.5), kind=kLoop, calls=%fused_computation | loop fusion | flops 512 | bytes 3072 | tf_op jit(solution)/shard_map/reshape | solution.py:278
Async XLA Ops:
  2.0 8.0 %collective-permute-start.3 = (bf16[776,128]{1,0:T(8,128)(2,1)S(1)}, bf16[776,128]{1,0:T(8,128)(2,1)S(1)}, u32[]{:S(2)}, u32[]{:S(2)}) collective-permute-start(bf16[776,128]{1,0:T(8,128)(2,1)S(1)} %shard_map.55.refs_0_.refs_4_), channel_id=1, source_target_pairs={{2,0},{3,1},{0,2},{1,3},{6,4},{7,5},{4,6},{5,7},{10,8},{11,9},{8,1... | collective-permute-start | bytes 595976 | tf_op jit(solution)/shard_map/ppermute | solution.py:253
  5.0 5.0 %collective-permute-start.2 = (bf16[776,128]{1,0:T(8,128)(2,1)S(1)}, bf16[776,128]{1,0:T(8,128)(2,1)S(1)}, u32[]{:S(2)}, u32[]{:S(2)}) collective-permute-start(bf16[776,128]{1,0:T(8,128)(2,1)S(1)} %shard_map.55.refs_0_.refs_4_), channel_id=1, source_target_pairs={{1,0},{0,1},{3,2},{2,3},{5,4},{4,5},{7,6},{6,7},{9,8},{8,9},{11,10... | collective-permute-start | bytes 595976 | tf_op jit(solution)/shard_map/ppermute | solution.py:253
  5.0 11.5 %collective-permute-start.1 = (bf16[776,128]{1,0:T(8,128)(2,1)S(1)}, bf16[776,128]{1,0:T(8,128)(2,1)S(1)}, u32[]{:S(2)}, u32[]{:S(2)}) collective-permute-start(bf16[776,128]{1,0:T(8,128)(2,1)S(1)} %shard_map.55.refs_0_.refs_4_), channel_id=1, source_target_pairs={{4,0},{5,1},{6,2},{7,3},{0,4},{1,5},{2,6},{3,7},{12,8},{13,9},{14,... | collective-permute-start | bytes 595976 | tf_op jit(solution)/shard_map/ppermute | solution.py:253
  6.6 12.3 %collective-permute-start = (bf16[776,128]{1,0:T(8,128)(2,1)S(1)}, bf16[776,128]{1,0:T(8,128)(2,1)S(1)}, u32[]{:S(2)}, u32[]{:S(2)}) collective-permute-start(bf16[776,128]{1,0:T(8,128)(2,1)S(1)} %shard_map.55.refs_0_.refs_4_), channel_id=1, source_target_pairs={{8,0},{9,1},{10,2},{11,3},{12,4},{13,5},{14,6},{15,7},{4,8},{5,9},... | collective-permute-start | bytes 595976 | tf_op jit(solution)/shard_map/ppermute | solution.py:253
  10.0 8.9 %collective-permute-start.4 = (bf16[776,128]{1,0:T(8,128)(2,1)S(1)}, bf16[776,128]{1,0:T(8,128)(2,1)S(1)}, u32[]{:S(2)}, u32[]{:S(2)}) collective-permute-start(bf16[776,128]{1,0:T(8,128)(2,1)S(1)} %collective-permute-done.3.refs_2_), channel_id=1, source_target_pairs={{1,0},{0,1},{3,2},{2,3},{5,4},{4,5},{7,6},{6,7},{9,8},{8,9},{11,10... | collective-permute-start | bytes 595976 | tf_op jit(solution)/shard_map/ppermute | solution.py:253
  19.3 4.5 %collective-permute-start.8 = (f32[1,128]{1,0:T(1,128)S(1)}, f32[1,128]{1,0:T(1,128)S(1)}, u32[]{:S(2)}, u32[]{:S(2)}) collective-permute-start(f32[1,128]{1,0:T(1,128)S(1)} %get-tuple-element.12), channel_id=1, source_target_pairs={{0,1},{1,0},{2,3},{3,2},{4,5},{5,4},{6,7},{7,6},{8,9},{9,8},{10,11... | collective-permute-start | bytes 1544 | tf_op jit(solution)/shard_map/ppermute | solution.py:253
  19.8 4.0 %collective-permute-start.6 = (f32[1,128]{1,0:T(1,128)S(1)}, f32[1,128]{1,0:T(1,128)S(1)}, u32[]{:S(2)}, u32[]{:S(2)}) collective-permute-start(f32[1,128]{1,0:T(1,128)S(1)} %get-tuple-element.10), channel_id=1, source_target_pairs={{0,2},{1,3},{2,0},{3,1},{4,6},{5,7},{6,4},{7,5},{8,10},{9,11},{10,... | collective-permute-start | bytes 1544 | tf_op jit(solution)/shard_map/ppermute | solution.py:253
  20.4 3.4 %collective-permute-start.7 = (f32[1,128]{1,0:T(1,128)S(1)}, f32[1,128]{1,0:T(1,128)S(1)}, u32[]{:S(2)}, u32[]{:S(2)}) collective-permute-start(f32[1,128]{1,0:T(1,128)S(1)} %get-tuple-element.11), channel_id=1, source_target_pairs={{0,3},{1,2},{2,1},{3,0},{4,7},{5,6},{6,5},{7,4},{8,11},{9,10},{10,... | collective-permute-start | bytes 1544 | tf_op jit(solution)/shard_map/ppermute | solution.py:253
  22.1 5.4 %collective-permute-start.5 = (f32[1,128]{1,0:T(1,128)S(1)}, f32[1,128]{1,0:T(1,128)S(1)}, u32[]{:S(2)}, u32[]{:S(2)}) collective-permute-start(f32[1,128]{1,0:T(1,128)S(1)} %shard_map.58), channel_id=1, source_target_pairs={{0,8},{1,9},{2,10},{3,11},{4,12},{5,13},{6,14},{7,15},{8,4},{9,5},... | collective-permute-start | bytes 1544 | tf_op jit(solution)/shard_map/ppermute | solution.py:253

commit v6 on v5

--- a/solution.py
+++ b/solution.py
@@ -172,7 +172,7 @@
 def embed(cls_feats, proj, cluster_id, row_index, assign, per_coarse):
     rows, depth = cls_feats.shape
     width = proj.shape[1]
-    chunks = 2
+    chunks = 4
     args = (cls_feats, proj, cluster_id.reshape(1, rows), row_index.reshape(1, rows), assign)
     return pl.pallas_call(
         functools.partial(embed_kernel, per_coarse),
@@ -258,7 +258,7 @@
     perms = [[(h[slot], d) for d, h in enumerate(sources)] for slot in range(FAR + 1)]
     early = [(q, c) for q, c in pairs if max(q, c) < PEER]
     rest = [(q, c) for q, c in pairs if q < FAR and max(q, c) >= PEER]
-    sooner, later = (PEER, SIDE), (OWN, CORE)
+    groups = {"beside": (PEER, SIDE), "core": (CORE,), "own": (OWN,)}
     own = embed(cls_feats, proj, cluster_id, row_index, assign, assign.shape[0] // n_dp)
     held = {slot: permute(own, perms[slot]) for slot in (FAR, NEAR, SIDE, CORE)}
     held[PEER] = permute(held[SIDE], perms[CORE])
@@ -266,7 +266,7 @@
     plane = {slot: held[slot] for slot in (OWN, CORE, SIDE, PEER)}
     best = scores({i: plane[i] for i in (OWN, CORE, SIDE)}, early, images)
     best |= scores(plane | {FAR: held[FAR]}, [(q, c) for q, c in pairs if q == FAR], images)
-    for group in (sooner, later):
+    for group in groups.values():
         part = [(q, c) for q, c in rest if q in group]
         used = {i: held[i] for i in held if any(i in pair for pair in part)}
         before = {OWN: best[OWN]} if OWN in group else {}

time: 28.2 us -> 28.1 us (level)
  waiting for transfers between devices: 13.2 us -> 12.8 us
    ppermute x9, waiting for transfers between devices: 13.2 us -> 12.8 us  [permute(): return lax.ppermute(value, GROUP, pairs)]
    pallas_call x4 -> x5, Pallas kernels: 1.53 us -> 1.72 us  [scores(): pl.pallas_call(functools.partial(score_kernel, images, len(names), wanted...]
  transfers between devices with their start and end apart: 9 -> 9, of which waited for: 4 -> 4; matrix products, arithmetic and copies ran while one was open for 0% -> 0% of each run, Pallas kernels for 4% -> 6%
where the time goes in v6:
time: 28.1 us; the launch traced here: 27.9 us
  waiting for transfers between devices  12.8 us (46%)
  starting transfers between devices  10.8 us (38%)
  Pallas kernels  3.75 us (13%)
  other arithmetic  0.52 us (2%)
    ppermute x9, waiting for transfers between devices, permute(): return lax.ppermute(value, GROUP, pairs)  12.8 us
    ppermute x9, starting transfers between devices, permute(): return lax.ppermute(value, GROUP, pairs)  10.8 us
    pallas_call x1, Pallas kernels, embed(): pl.pallas_call(functools.partial(embed_kernel, per_coarse), out_shape=jax...  2.03 us
    pallas_call x5, Pallas kernels, scores(): pl.pallas_call(functools.partial(score_kernel, images, len(names), wanted...  1.72 us
  transfers between devices with their start and end apart: 9, of which 4 were waited for; matrix products, arithmetic and copies ran while one was open for 0% of the time, Pallas kernels for 6%

profile of v6, /device:TPU:0, one launch (start us, length us, event | category | flops | bytes accessed | tf_op | source)
XLA Modules:
  0.0 27.9 jit_solution(1270832746678050884)
XLA Ops:
  0.0 2.0 %shard_map.55.refs_0_.refs_3_ = bf16[776,128]{1,0:T(8,128)(2,1)S(1)} custom-call(bf16[128,1024]{1,0:T(8,128)(2,1)} %cls_hbm.1, bf16[1024,768]{1,0:T(8,128)(2,1)} %proj_hbm.1, s32[1,128]{1,0:T(1,128)} %bitcast.4, s32[1,128]{1,0:T(1,128)} %bitcast.5, s32[8]{0:T(128)} %assign_hbm.1), custom_call_target="tpu_custom_call" | custom-call | tf_op jit(solution)/shard_map/pallas_call | solution.py:177
  2.0 3.0 %collective-permute-start.2 = (bf16[776,128]{1,0:T(8,128)(2,1)S(1)}, bf16[776,128]{1,0:T(8,128)(2,1)S(1)}, u32[]{:S(2)}, u32[]{:S(2)}) collective-permute-start(bf16[776,128]{1,0:T(8,128)(2,1)S(1)} %shard_map.55.refs_0_.refs_3_), channel_id=1, source_target_pairs={{2,0},{3,1},{0,2},{1,3},{6,4},{7,5},{4,6},{5,7},{10,8},{11,9},{8,1... | collective-permute-start | bytes 595976 | tf_op jit(solution)/shard_map/ppermute | solution.py:253
  5.1 0.0 collective-permute-start.4
  5.1 1.6 %collective-permute-start.1 = (bf16[776,128]{1,0:T(8,128)(2,1)S(1)}, bf16[776,128]{1,0:T(8,128)(2,1)S(1)}, u32[]{:S(2)}, u32[]{:S(2)}) collective-permute-start(bf16[776,128]{1,0:T(8,128)(2,1)S(1)} %shard_map.55.refs_0_.refs_3_), channel_id=1, source_target_pairs={{4,0},{5,1},{6,2},{7,3},{0,4},{1,5},{2,6},{3,7},{12,8},{13,9},{14,... | collective-permute-start | bytes 595976 | tf_op jit(solution)/shard_map/ppermute | solution.py:253
  6.7 2.5 %collective-permute-start = (bf16[776,128]{1,0:T(8,128)(2,1)S(1)}, bf16[776,128]{1,0:T(8,128)(2,1)S(1)}, u32[]{:S(2)}, u32[]{:S(2)}) collective-permute-start(bf16[776,128]{1,0:T(8,128)(2,1)S(1)} %shard_map.55.refs_0_.refs_3_), channel_id=1, source_target_pairs={{8,0},{9,1},{10,2},{11,3},{12,4},{13,5},{14,6},{15,7},{4,8},{5,9},... | collective-permute-start | bytes 595976 | tf_op jit(solution)/shard_map/ppermute | solution.py:253
  9.1 0.9 %collective-permute-done.2.refs_2_ = bf16[776,128]{1,0:T(8,128)(2,1)S(1)} collective-permute-done((bf16[776,128]{1,0:T(8,128)(2,1)S(1)}, bf16[776,128]{1,0:T(8,128)(2,1)S(1)}, u32[]{:S(2)}, u32[]{:S(2)}) %collective-permute-start.2) | collective-permute-done | bytes 198688 | tf_op jit(solution)/shard_map/ppermute | solution.py:253
  10.0 0.0 collective-permute-start.3
  10.0 0.0 collective-permute-done.4.refs_1_.refs_2_
  10.0 6.6 %collective-permute-done.1.refs_1_ = bf16[776,128]{1,0:T(8,128)(2,1)S(1)} collective-permute-done((bf16[776,128]{1,0:T(8,128)(2,1)S(1)}, bf16[776,128]{1,0:T(8,128)(2,1)S(1)}, u32[]{:S(2)}, u32[]{:S(2)}) %collective-permute-start.1) | collective-permute-done | bytes 198688 | tf_op jit(solution)/shard_map/ppermute | solution.py:253
  16.6 2.4 %collective-permute-done.refs_0_.refs_4_ = bf16[776,128]{1,0:T(8,128)(2,1)S(1)} collective-permute-done((bf16[776,128]{1,0:T(8,128)(2,1)S(1)}, bf16[776,128]{1,0:T(8,128)(2,1)S(1)}, u32[]{:S(2)}, u32[]{:S(2)}) %collective-permute-start) | collective-permute-done | bytes 198688 | tf_op jit(solution)/shard_map/ppermute | solution.py:253
  18.9 0.3 %shard_map.60 = f32[1,128]{1,0:T(1,128)S(1)} custom-call(bf16[776,128]{1,0:T(8,128)(2,1)S(1)} %collective-permute-done.refs_0_.refs_4_, bf16[776,128]{1,0:T(8,128)(2,1)S(1)} %collective-permute-done.1.refs_1_, bf16[776,128]{1,0:T(8,128)(2,1)S(1)} %collective-permute-done.4.refs_1_.refs_2_), custom_call_target="tpu_custom_call" | custom-call | tf_op jit(solution)/shard_map/pallas_call | solution.py:242
  19.2 0.1 collective-permute-start.8
  19.3 0.0 collective-permute-done.3.refs_2_.refs_3_
  19.3 0.4 %shard_map.59 = (f32[1,128]{1,0:T(1,128)S(1)}, f32[1,128]{1,0:T(1,128)S(1)}) custom-call(bf16[776,128]{1,0:T(8,128)(2,1)S(1)} %collective-permute-done.refs_0_.refs_4_, bf16[776,128]{1,0:T(8,128)(2,1)S(1)} %collective-permute-done.1.refs_1_, bf16[776,128]{1,0:T(8,128)(2,1)S(1)} %collective-permute-done.2.refs_2_, ...), custom_call_target="tpu_custom_call" | custom-call | tf_op jit(solution)/shard_map/pallas_call | solution.py:242
  19.7 0.6 %collective-permute-start.6 = (f32[1,128]{1,0:T(1,128)S(1)}, f32[1,128]{1,0:T(1,128)S(1)}, u32[]{:S(2)}, u32[]{:S(2)}) collective-permute-start(f32[1,128]{1,0:T(1,128)S(1)} %get-tuple-element.7), channel_id=1, source_target_pairs={{0,2},{1,3},{2,0},{3,1},{4,6},{5,7},{6,4},{7,5},{8,10},{9,11},{10,... | collective-permute-start | bytes 1544 | tf_op jit(solution)/shard_map/ppermute | solution.py:253
  20.3 1.3 %collective-permute-start.7 = (f32[1,128]{1,0:T(1,128)S(1)}, f32[1,128]{1,0:T(1,128)S(1)}, u32[]{:S(2)}, u32[]{:S(2)}) collective-permute-start(f32[1,128]{1,0:T(1,128)S(1)} %get-tuple-element.8), channel_id=1, source_target_pairs={{0,3},{1,2},{2,1},{3,0},{4,7},{5,6},{6,5},{7,4},{8,11},{9,10},{10,... | collective-permute-start | bytes 1544 | tf_op jit(solution)/shard_map/ppermute | solution.py:253
  21.6 0.4 %shard_map.58 = f32[1,128]{1,0:T(1,128)S(1)} custom-call(bf16[776,128]{1,0:T(8,128)(2,1)S(1)} %shard_map.55.refs_0_.refs_3_, bf16[776,128]{1,0:T(8,128)(2,1)S(1)} %collective-permute-done.4.refs_1_.refs_2_, bf16[776,128]{1,0:T(8,128)(2,1)S(1)} %collective-permute-done.2.refs_2_, bf16[776,128]{1,0:T(8,128)(2,1)S(1)} %collective-permute-done.3.refs_2_.refs_3_, ...), custom_call_target="tpu_custom_call" | custom-call | tf_op jit(solution)/shard_map/pallas_call | solution.py:242
  22.0 1.7 %collective-permute-start.5 = (f32[1,128]{1,0:T(1,128)S(1)}, f32[1,128]{1,0:T(1,128)S(1)}, u32[]{:S(2)}, u32[]{:S(2)}) collective-permute-start(f32[1,128]{1,0:T(1,128)S(1)} %shard_map.58), channel_id=1, source_target_pairs={{0,8},{1,9},{2,10},{3,11},{4,12},{5,13},{6,14},{7,15},{8,4},{9,5},... | collective-permute-start | bytes 1544 | tf_op jit(solution)/shard_map/ppermute | solution.py:253
  23.7 0.3 %shard_map.56.refs_4_ = f32[1,128]{1,0:T(1,128)S(1)} custom-call(bf16[776,128]{1,0:T(8,128)(2,1)S(1)} %shard_map.55.refs_0_.refs_3_, bf16[776,128]{1,0:T(8,128)(2,1)S(1)} %collective-permute-done.4.refs_1_.refs_2_, bf16[776,128]{1,0:T(8,128)(2,1)S(1)} %collective-permute-done.2.refs_2_), custom_call_target="tpu_custom_call" | custom-call | tf_op jit(solution)/shard_map/pallas_call | solution.py:242
  24.0 0.3 %shard_map.57 = f32[1,128]{1,0:T(1,128)S(1)} custom-call(bf16[776,128]{1,0:T(8,128)(2,1)S(1)} %collective-permute-done.refs_0_.refs_4_, bf16[776,128]{1,0:T(8,128)(2,1)S(1)} %collective-permute-done.1.refs_1_, bf16[776,128]{1,0:T(8,128)(2,1)S(1)} %collective-permute-done.3.refs_2_.refs_3_, bf16[776,128]{1,0:T(8,128)(2,1)S(1)} %shard_map.55.refs_0_.refs_3_, ...), custom_call_target="tpu_custom_call" | custom-call | tf_op jit(solution)/shard_map/pallas_call | solution.py:242
  24.4 0.0 collective-permute-done.8
  24.4 0.0 collective-permute-done.6
  24.4 0.0 collective-permute-done.7
  24.4 3.0 %collective-permute-done.5 = f32[1,128]{1,0:T(1,128)S(1)} collective-permute-done((f32[1,128]{1,0:T(1,128)S(1)}, f32[1,128]{1,0:T(1,128)S(1)}, u32[]{:S(2)}, u32[]{:S(2)}) %collective-permute-start.5) | collective-permute-done | bytes 544 | tf_op jit(solution)/shard_map/ppermute | solution.py:253
  27.4 0.5 %maximum_bitcast_fusion = f32[128]{0:T(128)} fusion(f32[1,128]{1,0:T(1,128)S(1)} %collective-permute-done.8, f32[1,128]{1,0:T(1,128)S(1)} %collective-permute-done.7, f32[1,128]{1,0:T(1,128)S(1)} %collective-permute-done.6, f32[1,128]{1,0:T(1,128)S(1)} %shard_map.57, f32[1,128]{1,0:T(1,128)S(1)} %collective-permute-done.5), kind=kLoop, calls=%fused_computation | loop fusion | flops 512 | bytes 3072 | tf_op jit(solution)/shard_map/reshape | solution.py:278
Async XLA Ops:
  2.0 8.0 %collective-permute-start.2 = (bf16[776,128]{1,0:T(8,128)(2,1)S(1)}, bf16[776,128]{1,0:T(8,128)(2,1)S(1)}, u32[]{:S(2)}, u32[]{:S(2)}) collective-permute-start(bf16[776,128]{1,0:T(8,128)(2,1)S(1)} %shard_map.55.refs_0_.refs_3_), channel_id=1, source_target_pairs={{2,0},{3,1},{0,2},{1,3},{6,4},{7,5},{4,6},{5,7},{10,8},{11,9},{8,1... | collective-permute-start | bytes 595976 | tf_op jit(solution)/shard_map/ppermute | solution.py:253
  5.1 5.0 %collective-permute-start.4 = (bf16[776,128]{1,0:T(8,128)(2,1)S(1)}, bf16[776,128]{1,0:T(8,128)(2,1)S(1)}, u32[]{:S(2)}, u32[]{:S(2)}) collective-permute-start(bf16[776,128]{1,0:T(8,128)(2,1)S(1)} %shard_map.55.refs_0_.refs_3_), channel_id=1, source_target_pairs={{1,0},{0,1},{3,2},{2,3},{5,4},{4,5},{7,6},{6,7},{9,8},{8,9},{11,10... | collective-permute-start | bytes 595976 | tf_op jit(solution)/shard_map/ppermute | solution.py:253
  5.1 11.5 %collective-permute-start.1 = (bf16[776,128]{1,0:T(8,128)(2,1)S(1)}, bf16[776,128]{1,0:T(8,128)(2,1)S(1)}, u32[]{:S(2)}, u32[]{:S(2)}) collective-permute-start(bf16[776,128]{1,0:T(8,128)(2,1)S(1)} %shard_map.55.refs_0_.refs_3_), channel_id=1, source_target_pairs={{4,0},{5,1},{6,2},{7,3},{0,4},{1,5},{2,6},{3,7},{12,8},{13,9},{14,... | collective-permute-start | bytes 595976 | tf_op jit(solution)/shard_map/ppermute | solution.py:253
  6.7 12.3 %collective-permute-start = (bf16[776,128]{1,0:T(8,128)(2,1)S(1)}, bf16[776,128]{1,0:T(8,128)(2,1)S(1)}, u32[]{:S(2)}, u32[]{:S(2)}) collective-permute-start(bf16[776,128]{1,0:T(8,128)(2,1)S(1)} %shard_map.55.refs_0_.refs_3_), channel_id=1, source_target_pairs={{8,0},{9,1},{10,2},{11,3},{12,4},{13,5},{14,6},{15,7},{4,8},{5,9},... | collective-permute-start | bytes 595976 | tf_op jit(solution)/shard_map/ppermute | solution.py:253
  10.0 9.3 %collective-permute-start.3 = (bf16[776,128]{1,0:T(8,128)(2,1)S(1)}, bf16[776,128]{1,0:T(8,128)(2,1)S(1)}, u32[]{:S(2)}, u32[]{:S(2)}) collective-permute-start(bf16[776,128]{1,0:T(8,128)(2,1)S(1)} %collective-permute-done.2.refs_2_), channel_id=1, source_target_pairs={{1,0},{0,1},{3,2},{2,3},{5,4},{4,5},{7,6},{6,7},{9,8},{8,9},{11,10... | collective-permute-start | bytes 595976 | tf_op jit(solution)/shard_map/ppermute | solution.py:253
  19.2 5.1 %collective-permute-start.8 = (f32[1,128]{1,0:T(1,128)S(1)}, f32[1,128]{1,0:T(1,128)S(1)}, u32[]{:S(2)}, u32[]{:S(2)}) collective-permute-start(f32[1,128]{1,0:T(1,128)S(1)} %shard_map.60), channel_id=1, source_target_pairs={{0,1},{1,0},{2,3},{3,2},{4,5},{5,4},{6,7},{7,6},{8,9},{9,8},{10,11... | collective-permute-start | bytes 1544 | tf_op jit(solution)/shard_map/ppermute | solution.py:253
  19.7 4.7 %collective-permute-start.6 = (f32[1,128]{1,0:T(1,128)S(1)}, f32[1,128]{1,0:T(1,128)S(1)}, u32[]{:S(2)}, u32[]{:S(2)}) collective-permute-start(f32[1,128]{1,0:T(1,128)S(1)} %get-tuple-element.7), channel_id=1, source_target_pairs={{0,2},{1,3},{2,0},{3,1},{4,6},{5,7},{6,4},{7,5},{8,10},{9,11},{10,... | collective-permute-start | bytes 1544 | tf_op jit(solution)/shard_map/ppermute | solution.py:253
  20.3 4.1 %collective-permute-start.7 = (f32[1,128]{1,0:T(1,128)S(1)}, f32[1,128]{1,0:T(1,128)S(1)}, u32[]{:S(2)}, u32[]{:S(2)}) collective-permute-start(f32[1,128]{1,0:T(1,128)S(1)} %get-tuple-element.8), channel_id=1, source_target_pairs={{0,3},{1,2},{2,1},{3,0},{4,7},{5,6},{6,5},{7,4},{8,11},{9,10},{10,... | collective-permute-start | bytes 1544 | tf_op jit(solution)/shard_map/ppermute | solution.py:253
  22.0 5.4 %collective-permute-start.5 = (f32[1,128]{1,0:T(1,128)S(1)}, f32[1,128]{1,0:T(1,128)S(1)}, u32[]{:S(2)}, u32[]{:S(2)}) collective-permute-start(f32[1,128]{1,0:T(1,128)S(1)} %shard_map.58), channel_id=1, source_target_pairs={{0,8},{1,9},{2,10},{3,11},{4,12},{5,13},{6,14},{7,15},{8,4},{9,5},... | collective-permute-start | bytes 1544 | tf_op jit(solution)/shard_map/ppermute | solution.py:253
